TPU v7x, 512 devices: a whole 4x4x16 slice. The times are simulated.
512 devices in a mesh: dom: 64 (over y, z), grp: 8 (over x, core).
Axes of the slice: x: 4, y: 4, z: 16, core: 2. Of those that a mesh axis runs over, the one named last changes fastest.
Arguments:
- source: float32 [2048, 256, 128], P('dom', 'grp'), may hold values from -48 to 48
- conductivity: float32 [2048, 256, 128], P('dom', 'grp'), may hold values from 0.3 to 3
- absorption: float32 [2048, 256, 128], P('dom', 'grp'), may hold values from 0.1 to 2
- brick_mask: int32 [256, 32, 16], P('dom', 'grp'), may hold values 0 or 1
Outputs:
- fine_iterate: float32 [2048, 256, 128], P('dom', 'grp')
- fine_residual: float32 [2048, 256, 128], P('dom', 'grp')
- mid_iterate: float32 [1024, 128, 64], P('dom', 'grp')
- coarse_iterate: float32 [512, 64, 32], P('dom', 'grp')
All inputs are finite; a program needn't handle non-finite values. No bound on the sum of `brick_mask` on one device may be relied on, other than what follows from the above.
Results may differ from a plain program's by a relative error of at most 0.00002.
Values sent between devices are 32-bit elements; how exact they have to be, the bound alone decides.
A program may use at most 192 MiB of HBM per device.

v0:
```python
import jax
import jax.numpy as jnp
from jax import lax
from jax.sharding import PartitionSpec as P

DEGREE = 4
COARSE_DEGREE = 6


step_scale = 4.0
smooth_low = 0.3
smooth_high = 2.0
coarse_low = 0.05


def extended_2(array, sides, width):
    for axis, dim in sides:
        devices, length = (lax.axis_size(axis), array.shape[dim])
        up = [(i, (i + 1) % devices) for i in range(devices - 1)]
        down = [(j, i) for i, j in up]
        last = lax.slice_in_dim(array, length - width, length, axis=dim)
        leading = lax.slice_in_dim(array, 0, width, axis=dim)
        before = lax.ppermute(last, axis, up)
        after = lax.ppermute(leading, axis, down)
        array = jnp.concatenate([before, array, after], axis=dim)
    return array


def refine_mask(brick_flags):
    values = brick_flags.astype(jnp.float32)
    values = jnp.repeat(values, 8, axis=0)
    values = jnp.repeat(values, 8, axis=1)
    return jnp.repeat(values, 8, axis=2)


def six_views(padded):
    return [
        padded[2:, 1:-1, 1:-1],
        padded[:-2, 1:-1, 1:-1],
        padded[1:-1, 2:, 1:-1],
        padded[1:-1, :-2, 1:-1],
        padded[1:-1, 1:-1, 2:],
        padded[1:-1, 1:-1, :-2],
    ]


def coefficients(kappa_pad, filled_pad, absorb_cells, factor):
    kappa_mid = kappa_pad[1:-1, 1:-1, 1:-1]
    weights = []
    summed = jnp.zeros_like(kappa_mid)
    counted = jnp.zeros_like(kappa_mid)
    for neighbour_kappa, neighbour_filled in zip(six_views(kappa_pad), six_views(filled_pad)):
        weight = factor * 0.5 * (kappa_mid + neighbour_kappa) * neighbour_filled
        weights.append(weight)
        summed = summed + weight
        counted = counted + neighbour_filled
    diagonal = 1.0 + summed + factor * absorb_cells * (6.0 - counted)
    return (weights, diagonal)


def apply_padded(field_pad, weights, diagonal, filled):
    center = field_pad[1:-1, 1:-1, 1:-1]
    neighbours = six_views(field_pad)
    coupled = weights[0] * neighbours[0]
    for index in range(1, 6):
        coupled = coupled + weights[index] * neighbours[index]
    return filled * (diagonal * center - coupled) + (1.0 - filled) * center


def chebyshev(source_term, diagonal, degree, lowest, highest, operate, keep_residual):
    middle = (highest + lowest) / 2.0
    spread = (highest - lowest) / 2.0
    relative = middle / spread
    factor_prev = 1.0 / relative
    inverse = 1.0 / diagonal
    update = inverse * source_term / middle
    iterate = update
    residual = source_term
    for sweep_index in range(degree):
        if sweep_index > 0:
            factor_next = 1.0 / (2.0 * relative - factor_prev)
            update = factor_next * factor_prev * update + 2.0 * factor_next / spread * (
                inverse * residual
            )
            iterate = iterate + update
            factor_prev = factor_next
        if sweep_index < degree - 1 or keep_residual:
            residual = residual - operate(update)
    return (iterate, residual)


def coarsen(fields):
    shape_in = fields.shape
    blocks = fields.reshape(shape_in[0] // 2, 2, shape_in[1] // 2, 2, shape_in[2] // 2, 2)
    return jnp.mean(blocks, axis=(1, 3, 5))


def margin_solve(extended, factor, degree, lowest, keep_residual, width):
    ext_pad = jnp.pad(extended, ((0, 0), (1, 1), (1, 1), (1, 1)))
    ext_filled = extended[3]
    weights, diagonal = coefficients(ext_pad[1], ext_pad[3], extended[2], factor)

    def operate(vector):
        return apply_padded(jnp.pad(vector, 1), weights, diagonal, ext_filled)

    long_iterate, long_residual = chebyshev(
        extended[0], diagonal, degree, lowest, smooth_high, operate, keep_residual
    )
    return (
        long_iterate[width:-width, width:-width, :],
        long_residual[width:-width, width:-width, :],
    )


def body(source, conductivity, absorption, brick_mask):
    filled = refine_mask(brick_mask)
    masked = source * filled
    margin_width = DEGREE + 1
    extended = extended_2(
        jnp.stack([masked, conductivity, absorption, filled]),
        (("dom", 1), ("grp", 2)),
        margin_width,
    )
    fine_iterate, fine_residual = margin_solve(
        extended, step_scale, DEGREE, smooth_low, True, margin_width
    )
    mid_kappa = coarsen(conductivity)
    mid_absorb = coarsen(absorption)
    mid_filled = coarsen(filled)
    mid_source = coarsen(fine_residual)
    coarse_kappa = coarsen(mid_kappa)
    coarse_absorb = coarsen(mid_absorb)
    coarse_filled = coarsen(mid_filled)
    coarse_factor = step_scale / 16.0
    mid_width = DEGREE + 1
    mid_ext = extended_2(
        jnp.stack([mid_source, mid_kappa, mid_absorb, mid_filled]),
        (("dom", 1), ("grp", 2)),
        mid_width,
    )
    mid_iterate, mid_residual = margin_solve(
        mid_ext, step_scale / 4.0, DEGREE, smooth_low, True, mid_width
    )
    coarse_width = COARSE_DEGREE
    coarse_ext = extended_2(
        jnp.stack([coarsen(mid_residual), coarse_kappa, coarse_absorb, coarse_filled]),
        (("dom", 1), ("grp", 2)),
        coarse_width,
    )
    coarse_iterate = margin_solve(
        coarse_ext, coarse_factor, COARSE_DEGREE, coarse_low, False, coarse_width
    )[0]
    return (fine_iterate, fine_residual, mid_iterate, coarse_iterate)


def solution(mesh):
    return jax.shard_map(
        body,
        mesh=mesh,
        in_specs=(
            P("dom", "grp", None),
            P("dom", "grp", None),
            P("dom", "grp", None),
            P("dom", "grp", None),
        ),
        out_specs=(
            P("dom", "grp", None),
            P("dom", "grp", None),
            P("dom", "grp", None),
            P("dom", "grp", None),
        ),
        check_vma=False,
    )
```

profile of v0, /device:TPU:25, one launch (start us, length us, event | category | flops | bytes accessed | tf_op | source)
XLA Modules:
  0.0 296.2 jit_solution(15284906449139357806)
XLA Ops:
  0.6 0.7 convert_element_type.25
  1.4 0.8 copy-done.8
  2.7 1.4 copy.28
  4.1 2.0 copy.26
  6.0 1.8 fusion.2
  7.9 1.4 copy.27
  9.3 1.9 pad_maximum_fusion.13
  11.2 3.5 %collective-permute-start = (f32[4,5,32,128]{3,2,1,0:T(8,128)}, f32[4,5,32,128]{3,2,1,0:T(8,128)S(1)}, u32[]{:S(2)}, u32[]{:S(2)}) collective-permute-start(f32[4,5,32,128]{3,2,1,0:T(8,128)} %get-tuple-element.57), channel_id=1, source_target_pairs={{0,8},{8,16},{16,24},{24,32},{32,40},{40,48},{48,56},{56,64},{64,7... | collective-permute-start | bytes 983048 | tf_op jit(solution)/shard_map/ppermute | solution.py:23
  14.8 9.7 %collective-permute-start.1 = (f32[4,5,32,128]{3,2,1,0:T(8,128)}, f32[4,5,32,128]{3,2,1,0:T(8,128)S(1)}, u32[]{:S(2)}, u32[]{:S(2)}) collective-permute-start(f32[4,5,32,128]{3,2,1,0:T(8,128)} %get-tuple-element.58), channel_id=1, source_target_pairs={{8,0},{16,8},{24,16},{32,24},{40,32},{48,40},{56,48},{64,56},{72,6... | collective-permute-start | bytes 983048 | tf_op jit(solution)/shard_map/ppermute | solution.py:24
  24.4 34.9 %reshape.122 = f32[16,2,16,2,64,2]{5,4,3,2,1,0:T(8,128)} reshape(f32[32,32,128]{2,1,0:T(8,128)S(1)} %copy-done.1) | data formatting | bytes 1048576 | tf_op jit(solution)/shard_map/reshape | solution.py:94
  59.3 34.8 %reshape.123 = f32[16,2,16,2,64,2]{5,4,3,2,1,0:T(8,128)} reshape(f32[32,32,128]{2,1,0:T(8,128)S(1)} %copy-done) | data formatting | bytes 1048576 | tf_op jit(solution)/shard_map/reshape | solution.py:94
  94.2 4.6 %broadcast_in_dim.18 = f32[32,32,16,4]{3,2,1,0:T(8,128)} broadcast(f32[32,32,16]{2,1,0:T(8,128)S(1)} %copy-done.9), dimensions={0,1,2} | broadcast | bytes 327680 | tf_op jit(solution)/shard_map/broadcast_in_dim | solution.py:33
  98.7 6.7 %broadcast_in_dim.19 = f32[16,2,16,2,64]{4,3,2,1,0:T(2,128)S(1)} reshape(f32[32,32,16,4]{3,2,1,0:T(8,128)} %broadcast_in_dim.18) | data formatting | bytes 524288 | tf_op jit(solution)/shard_map/broadcast_in_dim | solution.py:33
  105.4 12.2 %reduce_sum.73 = f32[16,16,64]{2,1,0:T(8,128)S(1)} reduce(f32[16,2,16,2,64,2]{5,4,3,2,1,0:T(8,128)} %reshape.122, f32[]{:T(128)} %constant.27.clone.1), dimensions={1,3,5}, to_apply=%region_1.2 | reduce | flops 114688 | bytes 589828 | tf_op jit(solution)/shard_map/reduce_sum | solution.py:95
  117.7 5.7 %div.89 = f32[8,2,8,2,32,2]{5,4,3,2,1,0:T(8,128)} reshape(f32[16,16,64]{2,1,0:T(8,128)S(1)} %get-tuple-element.84) | data formatting | bytes 131072 | tf_op jit(solution)/shard_map/div | solution.py:95
  123.4 2.6 reduce_sum.77
  126.0 13.0 %reduce_sum.74 = f32[16,16,64]{2,1,0:T(8,128)} reduce(f32[16,2,16,2,64,2]{5,4,3,2,1,0:T(8,128)} %reshape.123, f32[]{:T(128)} %constant.27.clone.1), dimensions={1,3,5}, to_apply=%region_2.3 | reduce | flops 114688 | bytes 589828 | tf_op jit(solution)/shard_map/reduce_sum | solution.py:95
  139.1 0.9 copy.34
  140.1 0.9 copy.35
  141.0 2.9 collective-permute-start.3
  143.9 3.2 %collective-permute-start.2 = (f32[4,42,5,128]{3,0,2,1:T(4,128)}, f32[4,42,5,128]{3,0,2,1:T(4,128)}, u32[]{:S(2)}, u32[]{:S(2)}) collective-permute-start(f32[4,42,5,128]{3,0,2,1:T(4,128)} %copy.34), channel_id=1, source_target_pairs={{0,1},{1,2},{2,3},{3,4},{4,5},{5,6},{6,7},{8,9},{9,10},{10,11},{11... | collective-permute-start | bytes 1290248 | tf_op jit(solution)/shard_map/ppermute | solution.py:23
  147.1 0.8 broadcast_multiply_fusion
  147.8 5.7 %div.95 = f32[8,2,8,2,32,2]{5,4,3,2,1,0:T(8,128)} reshape(f32[16,16,64]{2,1,0:T(8,128)S(1)} %get-tuple-element.88) | data formatting | bytes 131072 | tf_op jit(solution)/shard_map/div | solution.py:95
  153.5 3.2 %reduce_sum.79 = f32[8,8,32]{2,1,0:T(8,128)} reduce(f32[8,2,8,2,32,2]{5,4,3,2,1,0:T(8,128)} %div.95, f32[]{:T(128)} %constant.27.clone.1), dimensions={1,3,5}, to_apply=%region_7.8 | reduce | flops 14336 | bytes 73732 | tf_op jit(solution)/shard_map/reduce_sum | solution.py:95
  156.7 1.1 copy.32
  157.8 1.1 copy.31
  158.9 2.0 pad_maximum_fusion
  160.9 1.0 slice_bitcast_fusion
  161.9 1.1 fusion
  163.1 3.2 %fusion.72 = (f32[42,42,128]{2,1,0:T(8,128)S(1)}, f32[42,42,128]{2,1,0:T(8,128)S(1)}, f32[42,42,128]{2,1,0:T(8,128)S(1)}, f32[42,42,128]{2,1,0:T(8,128)S(1)}, f3...) fusion(f32[4,42,42,128]{3,2,1,0:T(8,128)S(1)} %pad_maximum_fusi, ...), kind=kLoop, calls=%fused_computation.119 | loop fusion | flops 8128512 | bytes 20772864 | tf_op jit(solution)/shard_map/div | solution.py:76
  166.2 1.3 multiply_add_fusion.2
  167.5 2.4 multiply_add_fusion.1
  169.9 6.8 %multiply_add_fusion = (f32[42,42,128]{2,1,0:T(8,128)}, f32[42,42,128]{2,1,0:T(8,128)}, f32[42,42,128]{2,1,0:T(8,128)}) fusion(f32[42,42,128]{2,1,0:T(8,128)} %get-tuple-element.41, f32[42,42,128]{2,1,0:T(8,128)S(1)} %get-tuple-element.42, f32[42,42,128]{2,1,0:T(8,128)S(1)} %get-tuple-element.45, f32[42,42,128]{2,1,0:T(8,128)} %get-tuple-element.40, ...), kind=kLoop, calls=%fused_computation.114 | loop fusion | flops 6096384 | bytes 12644352 | tf_op jit(solution)/shard_map/add | solution.py:82
  176.7 4.2 %fusion.51 = (f32[42,42,128]{2,1,0:T(8,128)S(1)}, f32[42,42,128]{2,1,0:T(8,128)S(1)}, f32[42,42,128]{2,1,0:T(8,128)S(1)}) fusion(f32[42,42,128]{2,1,0:T(8,128)S(1)} %get-tuple-element.51, f32[42,42,128]{2,1,0:T(8,128)} %get-tuple-element.38, f32[42,42,128]{2,1,0:T(8,128)S(1)} %get-tuple-element.46, f32[42,42,128]{2,1,0:T(8,128)S(1)} %get-tuple-element.47, ...), kind=kLoop, calls=%fused_computation.85 | loop fusion | flops 1806336 | bytes 8128512 | tf_op jit(solution)/shard_map/add | solution.py:66
  181.3 1.4 slice_subtract_fusion
  182.7 34.8 %reshape.121 = f32[16,2,16,2,64,2]{5,4,3,2,1,0:T(8,128)} reshape(f32[32,32,128]{2,1,0:T(8,128)S(1)} %get-tuple-element.64) | data formatting | bytes 1048576 | tf_op jit(solution)/shard_map/reshape | solution.py:94
  217.6 12.3 %reduce_sum.72 = f32[16,16,64]{2,1,0:T(8,128)S(1)} reduce(f32[16,2,16,2,64,2]{5,4,3,2,1,0:T(8,128)} %reshape.121, f32[]{:T(128)} %constant.27.clone.1), dimensions={1,3,5}, to_apply=%region_0.1 | reduce | flops 114688 | bytes 589828 | tf_op jit(solution)/shard_map/reduce_sum | solution.py:95
  229.9 1.9 collective-permute-start.4
  231.8 5.5 %collective-permute-start.5 = (f32[4,5,16,64]{3,2,1,0:T(8,128)S(1)}, f32[4,5,16,64]{3,2,1,0:T(8,128)S(1)}, u32[]{:S(2)}, u32[]{:S(2)}) collective-permute-start(f32[4,5,16,64]{3,2,1,0:T(8,128)S(1)} %get-tuple-element.74), channel_id=1, source_target_pairs={{8,0},{16,8},{24,16},{32,24},{40,32},{48,40},{56,48},{64,56},{72,6... | collective-permute-start | bytes 245768 | tf_op jit(solution)/shard_map/ppermute | solution.py:24
  237.3 5.7 %div.92 = f32[8,2,8,2,32,2]{5,4,3,2,1,0:T(8,128)} reshape(f32[16,16,64]{2,1,0:T(8,128)S(1)} %copy-done.18) | data formatting | bytes 131072 | tf_op jit(solution)/shard_map/div | solution.py:95
  243.0 2.6 reduce_sum.78
  245.7 3.0 %collective-permute-start.6 = (f32[4,26,5,64]{3,2,1,0:T(8,128)S(1)}, f32[4,26,5,64]{3,2,1,0:T(8,128)S(1)}, u32[]{:S(2)}, u32[]{:S(2)}) collective-permute-start(f32[4,26,5,64]{3,2,1,0:T(8,128)S(1)} %get-tuple-element.71), channel_id=1, source_target_pairs={{0,1},{1,2},{2,3},{3,4},{4,5},{5,6},{6,7},{8,9},{9,10},{10,11},{11... | collective-permute-start | bytes 399368 | tf_op jit(solution)/shard_map/ppermute | solution.py:23
  248.7 1.9 collective-permute-start.7
  250.7 3.1 %collective-permute-done.6 = f32[4,26,5,64]{3,2,1,0:T(8,128)S(1)} collective-permute-done((f32[4,26,5,64]{3,2,1,0:T(8,128)S(1)}, f32[4,26,5,64]{3,2,1,0:T(8,128)S(1)}, u32[]{:S(2)}, u32[]{:S(2)}) %collective-permute-start.6) | collective-permute-done | bytes 133152 | tf_op jit(solution)/shard_map/ppermute | solution.py:23
  253.8 4.4 %collective-permute-done.7 = f32[4,26,5,64]{3,2,1,0:T(8,128)S(1)} collective-permute-done((f32[4,26,5,64]{3,2,1,0:T(8,128)S(1)}, f32[4,26,5,64]{3,2,1,0:T(8,128)S(1)}, u32[]{:S(2)}, u32[]{:S(2)}) %collective-permute-start.7) | collective-permute-done | bytes 133152 | tf_op jit(solution)/shard_map/ppermute | solution.py:24
  258.8 1.3 fusion.116
  260.1 0.7 multiply_add_fusion.6
  260.8 0.7 multiply_add_fusion.5
  261.4 0.7 multiply_add_fusion.4
  262.1 0.5 multiply_add_fusion.3
  262.6 0.9 slice_subtract_fusion.1
  263.5 5.7 %reshape.124 = f32[8,2,8,2,32,2]{5,4,3,2,1,0:T(8,128)} reshape(f32[16,16,64]{2,1,0:T(8,128)S(1)} %get-tuple-element.75) | data formatting | bytes 131072 | tf_op jit(solution)/shard_map/reshape | solution.py:94
  269.2 2.6 reduce_sum.76
  271.8 1.9 collective-permute-start.8
  273.7 5.5 %collective-permute-start.9 = (f32[4,6,8,32]{3,2,1,0:T(8,128)S(1)}, f32[4,6,8,32]{3,2,1,0:T(8,128)S(1)}, u32[]{:S(2)}, u32[]{:S(2)}) collective-permute-start(f32[4,6,8,32]{3,2,1,0:T(8,128)S(1)} %get-tuple-element.83), channel_id=1, source_target_pairs={{8,0},{16,8},{24,16},{32,24},{40,32},{48,40},{56,48},{64,56},{72,6... | collective-permute-start | bytes 73736 | tf_op jit(solution)/shard_map/ppermute | solution.py:24
  279.3 1.6 collective-permute-done.9
  280.9 3.3 %collective-permute-start.10 = (f32[4,20,6,32]{3,2,1,0:T(8,128)S(1)}, f32[4,20,6,32]{3,2,1,0:T(8,128)S(1)}, u32[]{:S(2)}, u32[]{:S(2)}) collective-permute-start(f32[4,20,6,32]{3,2,1,0:T(8,128)S(1)} %get-tuple-element.80), channel_id=1, source_target_pairs={{0,1},{1,2},{2,3},{3,4},{4,5},{5,6},{6,7},{8,9},{9,10},{10,11},{11... | collective-permute-start | bytes 184328 | tf_op jit(solution)/shard_map/ppermute | solution.py:23
  284.2 2.2 collective-permute-start.11
  286.4 1.8 collective-permute-done.10
  288.2 4.4 %collective-permute-done.11 = f32[4,20,6,32]{3,2,1,0:T(8,128)S(1)} collective-permute-done((f32[4,20,6,32]{3,2,1,0:T(8,128)S(1)}, f32[4,20,6,32]{3,2,1,0:T(8,128)S(1)}, u32[]{:S(2)}, u32[]{:S(2)}) %collective-permute-start.11) | collective-permute-done | bytes 61472 | tf_op jit(solution)/shard_map/ppermute | solution.py:24
  293.0 0.8 broadcast_divide_fusion.2
  294.2 0.4 multiply_add_fusion.9
  294.5 0.4 multiply_add_fusion.8
  295.6 0.7 fusion.216
  (75 shorter events, 3.5 us)
Async XLA Ops:
  1.4 0.8 copy-start.8
  2.4 1.6 copy-start.17
  7.9 1.4 copy-start
  7.9 1.4 copy-start.1
  11.2 127.8 %collective-permute-start = (f32[4,5,32,128]{3,2,1,0:T(8,128)}, f32[4,5,32,128]{3,2,1,0:T(8,128)S(1)}, u32[]{:S(2)}, u32[]{:S(2)}) collective-permute-start(f32[4,5,32,128]{3,2,1,0:T(8,128)} %get-tuple-element.57), channel_id=1, source_target_pairs={{0,8},{8,16},{16,24},{24,32},{32,40},{40,48},{48,56},{56,64},{64,7... | collective-permute-start | bytes 983048 | tf_op jit(solution)/shard_map/ppermute | solution.py:23
  14.8 124.3 %collective-permute-start.1 = (f32[4,5,32,128]{3,2,1,0:T(8,128)}, f32[4,5,32,128]{3,2,1,0:T(8,128)S(1)}, u32[]{:S(2)}, u32[]{:S(2)}) collective-permute-start(f32[4,5,32,128]{3,2,1,0:T(8,128)} %get-tuple-element.58), channel_id=1, source_target_pairs={{8,0},{16,8},{24,16},{32,24},{40,32},{48,40},{56,48},{64,56},{72,6... | collective-permute-start | bytes 983048 | tf_op jit(solution)/shard_map/ppermute | solution.py:24
  59.3 34.8 %copy-start.9 = (f32[32,32,16]{2,1,0:T(8,128)S(1)}, f32[32,32,16]{2,1,0:T(8,128)}, u32[]{:S(2)}) copy-start(f32[32,32,16]{2,1,0:T(8,128)} %copy-done.8) | copy-start | bytes 196612
  125.9 13.1 %copy-start.2 = (f32[1,32,32,128]{3,2,1,0:T(8,128)S(1)}, f32[1,32,32,128]{3,2,1,0:T(8,128)}, u32[]{:S(2)}) copy-start(f32[1,32,32,128]{3,2,1,0:T(8,128)} %copy.28) | copy-start | bytes 1572868
  125.9 13.1 %copy-start.3 = (f32[1,32,32,128]{3,2,1,0:T(8,128)S(1)}, f32[1,32,32,128]{3,2,1,0:T(8,128)}, u32[]{:S(2)}) copy-start(f32[1,32,32,128]{3,2,1,0:T(8,128)} %copy.27) | copy-start | bytes 1572868
  139.0 8.1 %copy-start.16 = (f32[16,16,64]{2,1,0:T(8,128)S(1)}, f32[16,16,64]{2,1,0:T(8,128)}, u32[]{:S(2)}) copy-start(f32[16,16,64]{2,1,0:T(8,128)} %reduce_sum.74) | copy-start | bytes 196612
  141.0 15.7 %collective-permute-start.3 = (f32[4,42,5,128]{3,0,2,1:T(4,128)}, f32[4,42,5,128]{3,0,2,1:T(4,128)}, u32[]{:S(2)}, u32[]{:S(2)}) collective-permute-start(f32[4,42,5,128]{3,0,2,1:T(4,128)} %copy.35), channel_id=1, source_target_pairs={{1,0},{2,1},{3,2},{4,3},{5,4},{6,5},{7,6},{9,8},{10,9},{11,10},{12... | collective-permute-start | bytes 1290248 | tf_op jit(solution)/shard_map/ppermute | solution.py:24
  143.9 13.9 %collective-permute-start.2 = (f32[4,42,5,128]{3,0,2,1:T(4,128)}, f32[4,42,5,128]{3,0,2,1:T(4,128)}, u32[]{:S(2)}, u32[]{:S(2)}) collective-permute-start(f32[4,42,5,128]{3,0,2,1:T(4,128)} %copy.34), channel_id=1, source_target_pairs={{0,1},{1,2},{2,3},{3,4},{4,5},{5,6},{6,7},{8,9},{9,10},{10,11},{11... | collective-permute-start | bytes 1290248 | tf_op jit(solution)/shard_map/ppermute | solution.py:23
  166.2 1.3 copy-start.4
  176.7 4.2 %copy-start.5 = (f32[42,42,128]{2,1,0:T(8,128)S(1)}, f32[42,42,128]{2,1,0:T(8,128)}, u32[]{:S(2)}) copy-start(f32[42,42,128]{2,1,0:T(8,128)} %copy-done.4) | copy-start | bytes 2709508
  176.7 4.2 %copy-start.6 = (f32[42,42,128]{2,1,0:T(8,128)S(1)}, f32[42,42,128]{2,1,0:T(8,128)}, u32[]{:S(2)}) copy-start(f32[42,42,128]{2,1,0:T(8,128)} %get-tuple-element.40) | copy-start | bytes 2709508
  176.7 4.2 %copy-start.7 = (f32[42,42,128]{2,1,0:T(8,128)S(1)}, f32[42,42,128]{2,1,0:T(8,128)}, u32[]{:S(2)}) copy-start(f32[42,42,128]{2,1,0:T(8,128)} %get-tuple-element.38) | copy-start | bytes 2709508
  176.7 4.3 %copy-start.10 = (f32[42,42,128]{2,1,0:T(8,128)S(1)}, f32[42,42,128]{2,1,0:T(8,128)}, u32[]{:S(2)}) copy-start(f32[42,42,128]{2,1,0:T(8,128)} %get-tuple-element.39) | copy-start | bytes 2709508
  176.7 4.3 %copy-start.11 = (f32[42,42,128]{2,1,0:T(8,128)S(1)}, f32[42,42,128]{2,1,0:T(8,128)}, u32[]{:S(2)}) copy-start(f32[42,42,128]{2,1,0:T(8,128)} %get-tuple-element.52) | copy-start | bytes 2709508
  176.7 4.6 %copy-start.12 = (f32[42,42,128]{2,1,0:T(8,128)S(1)}, f32[42,42,128]{2,1,0:T(8,128)}, u32[]{:S(2)}) copy-start(f32[42,42,128]{2,1,0:T(8,128)} %slice_bitcast_fusion) | copy-start | bytes 2709508
  182.7 34.8 %copy-start.13 = (f32[32,32,128]{2,1,0:T(8,128)}, f32[32,32,128]{2,1,0:T(8,128)S(1)}, u32[]{:S(2)}) copy-start(f32[32,32,128]{2,1,0:T(8,128)S(1)} %get-tuple-element.64) | copy-start | bytes 1572868
  217.5 12.3 %copy-start.14 = (f32[1,16,16,64]{3,2,1,0:T(8,128)S(1)}, f32[1,16,16,64]{3,2,1,0:T(8,128)}, u32[]{:S(2)}) copy-start(f32[1,16,16,64]{3,2,1,0:T(8,128)} %get-tuple-element.89) | copy-start | bytes 196612
  217.5 12.3 %copy-start.15 = (f32[1,16,16,64]{3,2,1,0:T(8,128)S(1)}, f32[1,16,16,64]{3,2,1,0:T(8,128)}, u32[]{:S(2)}) copy-start(f32[1,16,16,64]{3,2,1,0:T(8,128)} %get-tuple-element.90) | copy-start | bytes 196612
  217.5 19.8 %copy-start.19 = (f32[8,8,32]{2,1,0:T(8,128)S(1)}, f32[8,8,32]{2,1,0:T(8,128)}, u32[]{:S(2)}) copy-start(f32[8,8,32]{2,1,0:T(8,128)} %reduce_sum.79) | copy-start | bytes 24580
  217.6 19.8 %copy-start.18 = (f32[16,16,64]{2,1,0:T(8,128)S(1)}, f32[16,16,64]{2,1,0:T(8,128)}, u32[]{:S(2)}) copy-start(f32[16,16,64]{2,1,0:T(8,128)} %get-tuple-element.91) | copy-start | bytes 196612
  229.9 15.7 %collective-permute-start.4 = (f32[4,5,16,64]{3,2,1,0:T(8,128)S(1)}, f32[4,5,16,64]{3,2,1,0:T(8,128)S(1)}, u32[]{:S(2)}, u32[]{:S(2)}) collective-permute-start(f32[4,5,16,64]{3,2,1,0:T(8,128)S(1)} %get-tuple-element.73), channel_id=1, source_target_pairs={{0,8},{8,16},{16,24},{24,32},{32,40},{40,48},{48,56},{56,64},{64,7... | collective-permute-start | bytes 245768 | tf_op jit(solution)/shard_map/ppermute | solution.py:23
  231.8 13.8 %collective-permute-start.5 = (f32[4,5,16,64]{3,2,1,0:T(8,128)S(1)}, f32[4,5,16,64]{3,2,1,0:T(8,128)S(1)}, u32[]{:S(2)}, u32[]{:S(2)}) collective-permute-start(f32[4,5,16,64]{3,2,1,0:T(8,128)S(1)} %get-tuple-element.74), channel_id=1, source_target_pairs={{8,0},{16,8},{24,16},{32,24},{40,32},{48,40},{56,48},{64,56},{72,6... | collective-permute-start | bytes 245768 | tf_op jit(solution)/shard_map/ppermute | solution.py:24
  245.7 8.0 %collective-permute-start.6 = (f32[4,26,5,64]{3,2,1,0:T(8,128)S(1)}, f32[4,26,5,64]{3,2,1,0:T(8,128)S(1)}, u32[]{:S(2)}, u32[]{:S(2)}) collective-permute-start(f32[4,26,5,64]{3,2,1,0:T(8,128)S(1)} %get-tuple-element.71), channel_id=1, source_target_pairs={{0,1},{1,2},{2,3},{3,4},{4,5},{5,6},{6,7},{8,9},{9,10},{10,11},{11... | collective-permute-start | bytes 399368 | tf_op jit(solution)/shard_map/ppermute | solution.py:23
  248.7 9.4 %collective-permute-start.7 = (f32[4,26,5,64]{3,2,1,0:T(8,128)S(1)}, f32[4,26,5,64]{3,2,1,0:T(8,128)S(1)}, u32[]{:S(2)}, u32[]{:S(2)}) collective-permute-start(f32[4,26,5,64]{3,2,1,0:T(8,128)S(1)} %get-tuple-element.72), channel_id=1, source_target_pairs={{1,0},{2,1},{3,2},{4,3},{5,4},{6,5},{7,6},{9,8},{10,9},{11,10},{12... | collective-permute-start | bytes 399368 | tf_op jit(solution)/shard_map/ppermute | solution.py:24
  271.8 7.5 %collective-permute-start.8 = (f32[4,6,8,32]{3,2,1,0:T(8,128)S(1)}, f32[4,6,8,32]{3,2,1,0:T(8,128)S(1)}, u32[]{:S(2)}, u32[]{:S(2)}) collective-permute-start(f32[4,6,8,32]{3,2,1,0:T(8,128)S(1)} %get-tuple-element.82), channel_id=1, source_target_pairs={{0,8},{8,16},{16,24},{24,32},{32,40},{40,48},{48,56},{56,64},{64,7... | collective-permute-start | bytes 73736 | tf_op jit(solution)/shard_map/ppermute | solution.py:23
  273.7 7.1 %collective-permute-start.9 = (f32[4,6,8,32]{3,2,1,0:T(8,128)S(1)}, f32[4,6,8,32]{3,2,1,0:T(8,128)S(1)}, u32[]{:S(2)}, u32[]{:S(2)}) collective-permute-start(f32[4,6,8,32]{3,2,1,0:T(8,128)S(1)} %get-tuple-element.83), channel_id=1, source_target_pairs={{8,0},{16,8},{24,16},{32,24},{40,32},{48,40},{56,48},{64,56},{72,6... | collective-permute-start | bytes 73736 | tf_op jit(solution)/shard_map/ppermute | solution.py:24
  280.9 7.3 %collective-permute-start.10 = (f32[4,20,6,32]{3,2,1,0:T(8,128)S(1)}, f32[4,20,6,32]{3,2,1,0:T(8,128)S(1)}, u32[]{:S(2)}, u32[]{:S(2)}) collective-permute-start(f32[4,20,6,32]{3,2,1,0:T(8,128)S(1)} %get-tuple-element.80), channel_id=1, source_target_pairs={{0,1},{1,2},{2,3},{3,4},{4,5},{5,6},{6,7},{8,9},{9,10},{10,11},{11... | collective-permute-start | bytes 184328 | tf_op jit(solution)/shard_map/ppermute | solution.py:23
  284.2 8.4 %collective-permute-start.11 = (f32[4,20,6,32]{3,2,1,0:T(8,128)S(1)}, f32[4,20,6,32]{3,2,1,0:T(8,128)S(1)}, u32[]{:S(2)}, u32[]{:S(2)}) collective-permute-start(f32[4,20,6,32]{3,2,1,0:T(8,128)S(1)} %get-tuple-element.81), channel_id=1, source_target_pairs={{1,0},{2,1},{3,2},{4,3},{5,4},{6,5},{7,6},{9,8},{10,9},{11,10},{12... | collective-permute-start | bytes 184328 | tf_op jit(solution)/shard_map/ppermute | solution.py:24
where the time goes:
time: 297 us; the launch traced here: 296 us
  local copies, waits for them, and re-layouts  152 us (51%)
  other arithmetic  83.4 us (28%)
  starting transfers between devices  44.4 us (15%)
  waiting for transfers between devices  15.3 us (5%)
    reshape x4, local copies, waits for them, and re-layouts, coarsen(): fields.reshape(shape_in[0] // 2, 2, shape_in[1] // 2, 2, shape_in[2] // 2...  110 us
    reduce_sum x8, other arithmetic, coarsen(): return jnp.mean(blocks, axis=(1, 3, 5))  48.3 us
    ppermute x6, starting transfers between devices, extended_2(): after = lax.ppermute(leading, axis, down)  27.6 us
    div x3, local copies, waits for them, and re-layouts, coarsen(): return jnp.mean(blocks, axis=(1, 3, 5))  17 us
    ppermute x6, starting transfers between devices, extended_2(): before = lax.ppermute(last, axis, up)  16.9 us
    add x10, other arithmetic, chebyshev(): factor_next * factor_prev * update  13.8 us
    broadcast_in_dim x3, local copies, waits for them, and re-layouts, refine_mask(): return jnp.repeat(values, 8, axis=2)  11.3 us
    ppermute x6, waiting for transfers between devices, extended_2(): after = lax.ppermute(leading, axis, down)  10.4 us
  transfers between devices with their start and end apart: 12, of which 6 were waited for; matrix products, arithmetic and copies ran while one was open for 45% of the time, Pallas kernels for 0%

commit v1 on v0

v1 whole, which is shorter than its diff:
```python
import jax
import jax.numpy as jnp
from jax import lax
from jax.experimental import pallas as pl
from jax.experimental.pallas import tpu as pltpu
from jax.sharding import PartitionSpec as P

DEGREE = 4
COARSE_DEGREE = 6
STEP_SCALE = 4.0
SMOOTH_LOW = 0.3
SMOOTH_HIGH = 2.0
COARSE_LOW = 0.05
LANES = 128
MESH = pl.DeviceIdType.MESH
DIRS = tuple((a, b) for a in (-1, 0, 1) for b in (-1, 0, 1) if (a, b) != (0, 0))
F32 = jnp.float32


def recurrence(degree, lowest, highest):
    middle = (highest + lowest) / 2.0
    spread = (highest - lowest) / 2.0
    relative = middle / spread
    factor = 1.0 / relative
    steps = []
    for _ in range(degree - 1):
        following = 1.0 / (2.0 * relative - factor)
        steps.append((following * factor, 2.0 * following / spread))
        factor = following
    return 1.0 / middle, tuple(steps)


class Level:
    def __init__(self, n, margin, rows, stride, scale, degree, lowest):
        self.n, self.margin, self.stride, self.scale = n, margin, stride, scale
        self.nx = n + 2 * margin
        self.y0 = 8 - margin
        self.ny = rows
        self.yb = 8 * ((self.y0 + rows + 1 + 7) // 8)
        self.first, self.steps = recurrence(degree, lowest, SMOOTH_HIGH)
        self.degree = degree

    def coefficient_shape(self):
        return (self.n + 2 * self.margin + 2, self.yb, LANES)

    def source_shape(self):
        return (self.nx, self.yb, LANES)

    def work_shape(self):
        return (self.nx, self.ny + 16, LANES)


def span(sign, n, margin):
    if sign == 0:
        return 0, n
    return (n - margin, margin) if sign > 0 else (0, margin)


def landing(sign, n, margin, offset):
    if sign == 0:
        return offset
    return offset - margin if sign > 0 else offset + n


def lane_index():
    return lax.broadcasted_iota(jnp.int32, (1, LANES), 1)


def pool(read, write, count, stride):
    even = lax.rem(lane_index() // stride, 2) == 0

    def body(i, carry):
        p = (read(2 * i, 0) + read(2 * i, 1)) + (read(2 * i + 1, 0) + read(2 * i + 1, 1))
        other = jnp.where(even, pltpu.roll(p, LANES - stride, 1), pltpu.roll(p, stride, 1))
        write(i, (p + other) * 0.125)
        return carry

    lax.fori_loop(0, count, body, 0)


def setup(level, kappa, absorb, work):
    wx, wy, wz, diag, inv = work
    half = level.scale * 0.5
    up = lane_index() < LANES - level.stride
    down = lane_index() >= level.stride
    y0, ny = level.y0, level.ny

    def body(i, carry):
        k = kappa(i + 1, y0)
        xp, xm = kappa(i + 2, y0), kappa(i, y0)
        yp, ym = kappa(i + 1, y0 + 1), kappa(i + 1, y0 - 1)
        zp = jnp.where(up, pltpu.roll(k, LANES - level.stride, 1), 0.0)
        zm = jnp.where(down, pltpu.roll(k, level.stride, 1), 0.0)
        total = (xp + xm) + (yp + ym) + (zp + zm)
        count = jnp.zeros_like(k)
        for face in (xp, xm, yp, ym, zp, zm):
            count = count + jnp.where(face > 0.0, 1.0, 0.0)
        d = (1.0 + half * (k * count + total)) + level.scale * absorb(i, y0) * (6.0 - count)
        rows = pl.ds(8, ny)
        wx[i, rows, :] = half * (k + xp)
        wy[i, rows, :] = half * (k + yp)
        wz[i, rows, :] = jnp.where(up, half * (k + zp), 0.0)
        diag[i, rows, :] = d
        inv[i, rows, :] = jnp.where(k > 0.0, 1.0 / d, 0.0)
        return carry

    lax.fori_loop(0, level.nx, body, 0)


def start_iterate(level, source, inv, u0):
    rows = pl.ds(8, level.ny)

    def body(i, carry):
        u0[i, rows, :] = (inv[i, rows, :] * source(i, level.y0, level.ny)) * level.first
        return carry

    lax.fori_loop(0, level.nx, body, 0)


def residual_row(level, work, u, r, i, start, size):
    wx, wy, wz, diag, inv = work
    rows = pl.ds(start, size)
    c = u[i, rows, :]
    t = wx[i, rows, :] * u[i + 1, rows, :] + wx[i - 1, rows, :] * u[i - 1, rows, :]
    t = t + (wy[i, rows, :] * u[i, pl.ds(start + 1, size), :]
             + wy[i, pl.ds(start - 1, size), :] * u[i, pl.ds(start - 1, size), :])
    z = wz[i, rows, :]
    t = t + (z * pltpu.roll(c, LANES - level.stride, 1) + pltpu.roll(z * c, level.stride, 1))
    return (r - diag[i, rows, :] * c) + t, c


def sweeps(level, source, work, r, us, finish):
    inv = work[4]
    last = len(us) - 1
    m, n = level.margin, level.n
    for k in range(last):
        a, b = level.steps[k]

        def body(i, carry, k=k, a=a, b=b):
            rows = pl.ds(8, level.ny)
            old = source(i, level.y0, level.ny) if k == 0 else r[i, rows, :]
            new, c = residual_row(level, work, us[k], old, i, 8, level.ny)
            r[i, rows, :] = new
            us[k + 1][i, rows, :] = a * c + b * (inv[i, rows, :] * new)
            return carry

        lax.fori_loop(k + 1, level.nx - 1 - k, body, 0)

    own = 8 + m

    def body(i, carry):
        rows = pl.ds(own, n)
        new, c = residual_row(level, work, us[last], r[i, rows, :], i, own, n)
        total = us[0][i, rows, :]
        for u in us[1:-1]:
            total = total + u[i, rows, :]
        finish(i - m, new, total + c, c, inv[i, rows, :])
        return carry

    lax.fori_loop(m, m + n, body, 0)


def body_kernel(levels, s_in, k_in, a_in, b_in, it_out, res_out, mid_out, coarse_out,
                kf, sf, af, km, am, sm, kc, ac, sc, nb, bm, fm, midr, midi, coai,
                wf, wm, wc, rf, rm, rc, uf, um, uc, local, send, recv):
    fine, mid, coarse = levels
    d, g = lax.axis_index("dom"), lax.axis_index("grp")
    nd, ng = lax.axis_size("dom"), lax.axis_size("grp")

    loads = []
    for slot, (operand, buffer, off) in enumerate(
            ((k_in, kf, fine.margin + 1), (a_in, af, fine.margin), (s_in, sf, fine.margin))):
        copy = pltpu.make_async_copy(operand, buffer.at[pl.ds(off, fine.n), pl.ds(8, fine.n), :],
                                     local.at[slot])
        copy.start()
        loads.append(copy)

    def neighbour(dx, dg):
        return (lax.rem(d + (nd + dx), nd), lax.rem(g + (ng + dg), ng))

    barrier = pltpu.get_barrier_semaphore()
    for dx, dg in DIRS:
        pl.semaphore_signal(barrier, inc=1, device_id=neighbour(dx, dg), device_id_type=MESH)
    pl.semaphore_wait(barrier, len(DIRS))

    used = [0]

    def remote(src, dst, dx, dg):
        slot = used[0]
        used[0] += 1
        return pltpu.make_async_remote_copy(
            src_ref=src, dst_ref=dst, send_sem=send.at[slot], recv_sem=recv.at[slot],
            device_id=neighbour(dx, dg), device_id_type=MESH)

    def halo(src, dst, n, margin, offset, src_offset):
        copies = []
        for dx, dg in DIRS:
            sx, cx = span(dx, n, margin)
            sy, cy = span(dg, n, margin)
            ox, oy = src_offset
            copies.append(remote(
                src.at[pl.ds(sx + ox, cx), pl.ds(sy + oy, cy), :],
                dst.at[pl.ds(landing(dx, n, margin, offset), cx),
                       pl.ds(landing(dg, n, margin, 8), cy), :], dx, dg))
        for copy in copies:
            copy.start()
        return copies

    bricks = [remote(b_in, nb.at[slot], dx, dg) for slot, (dx, dg) in enumerate(DIRS)]
    for copy in bricks:
        copy.start()
    fine_k = halo(k_in, kf, fine.n, fine.margin + 1, fine.margin + 1, (0, 0))
    fine_a = halo(a_in, af, fine.n, fine.margin, fine.margin, (0, 0))
    fine_s = halo(s_in, sf, fine.n, fine.margin, fine.margin, (0, 0))

    lanes_of = (lax.broadcasted_iota(jnp.int32, (16, LANES), 1) // 8
                == lax.broadcasted_iota(jnp.int32, (16, LANES), 0)).astype(F32)
    bm[...] = jnp.zeros_like(bm)
    for bx in range(4):
        bm[pl.ds(8 * (1 + bx) + 1, 4), :] = b_in[bx].astype(F32)

    def spread_mask():
        fm[...] = jnp.dot(bm[...], lanes_of, preferred_element_type=F32)

    spread_mask()

    def mask_tile(x, row, t):
        flag = jnp.broadcast_to(fm[pl.ds(row + t, 1), :], (8, LANES))
        kf[x, pl.ds(8 * t, 8), :] = kf[x, pl.ds(8 * t, 8), :] * flag

    loads[0].wait()
    kx = fine.margin + 1

    def mask_own(x, carry):
        for t in range(1, 5):
            mask_tile(x + kx, 8 * (1 + x // 8), t)
        return carry

    lax.fori_loop(0, fine.n, mask_own, 0)
    loads[1].wait()
    loads[2].wait()

    def reader(ref, x0, count):
        return lambda x, y: ref[x + x0, pl.ds(8 + y, count, stride=2), :]

    def writer(ref, x0, count):
        def write(x, value):
            ref[x + x0, pl.ds(8, count), :] = value
        return write

    mx, cx = mid.margin + 1, coarse.margin + 1
    pool(reader(kf, kx, mid.n), writer(km, mx, mid.n), mid.n, fine.stride)
    pool(reader(af, fine.margin, mid.n), writer(am, mid.margin, mid.n), mid.n, fine.stride)
    pool(reader(km, mx, coarse.n), writer(kc, cx, coarse.n), coarse.n, mid.stride)
    pool(reader(am, mid.margin, coarse.n), writer(ac, coarse.margin, coarse.n), coarse.n, mid.stride)
    mid_k = halo(km, km, mid.n, mx, mx, (mx, 8))
    mid_a = halo(am, am, mid.n, mid.margin, mid.margin, (mid.margin, 8))
    coarse_k = halo(kc, kc, coarse.n, cx, cx, (cx, 8))
    coarse_a = halo(ac, ac, coarse.n, coarse.margin, coarse.margin, (coarse.margin, 8))

    inside = {-1: (d < nd - 1), 1: (d > 0), 0: None}
    inside_g = {-1: (g < ng - 1), 1: (g > 0), 0: None}
    keep_x = {s: 1.0 if v is None else v.astype(F32) for s, v in inside.items()}
    keep_y = {s: 1.0 if v is None else v.astype(F32) for s, v in inside_g.items()}
    for copy in bricks:
        copy.wait_recv()
    for slot, (dx, dg) in enumerate(DIRS):
        xs = {0: (0, 1, 2, 3), 1: (3,), -1: (0,)}[dx]
        ys, cy = {0: (0, 4), 1: (3, 1), -1: (0, 1)}[dg]
        for bx in xs:
            row = {0: 1 + bx, 1: 0, -1: 5}[dx]
            col = {0: 1, 1: 0, -1: 5}[dg]
            bm[pl.ds(8 * row + col, cy), :] = (
                nb[slot, bx, pl.ds(ys, cy), :].astype(F32) * (keep_x[dx] * keep_y[dg]))
    spread_mask()

    for copy in fine_k:
        copy.wait_recv()

    def mask_side(x, carry):
        for t in (0, 5):
            mask_tile(x + kx, 8 * (1 + x // 8), t)
        return carry

    lax.fori_loop(0, fine.n, mask_side, 0)

    def mask_ends(x, carry):
        for t in range(6):
            mask_tile(x, 0, t)
            mask_tile(x + kx + fine.n, 40, t)
        return carry

    lax.fori_loop(0, kx, mask_ends, 0)

    for copy in fine_a:
        copy.wait_recv()

    def at(ref, size):
        return lambda x, y: ref[x, pl.ds(y, size), :]

    def of(ref):
        return lambda x, y, size: ref[x, pl.ds(y, size), :]

    setup(fine, at(kf, fine.ny), at(af, fine.ny), wf)
    for copy in fine_s:
        copy.wait_recv()
    start_iterate(fine, of(sf), wf[4], uf[0])

    def fine_finish(x, new, total, c, inv):
        it_out[x] = total
        res_out[x] = jnp.where(inv > 0.0, new, 0.0)

    sweeps(fine, of(sf), wf, rf, uf, fine_finish)

    pool(lambda x, y: res_out[x, pl.ds(y, mid.n, stride=2), :], writer(sm, mid.margin, mid.n),
         mid.n, fine.stride)
    mid_s = halo(sm, sm, mid.n, mid.margin, mid.margin, (mid.margin, 8))

    def zero_outside(level, ref, copies):
        for copy in copies:
            copy.wait_recv()
        w = level.margin + 1

        def ends(x, carry):
            rows = pl.ds(0, level.yb)
            ref[x, rows, :] = ref[x, rows, :] * keep_x[1]
            ref[x + w + level.n, rows, :] = ref[x + w + level.n, rows, :] * keep_x[-1]
            return carry

        lax.fori_loop(0, w, ends, 0)

        def edges(x, carry):
            ref[x, pl.ds(0, 8), :] = ref[x, pl.ds(0, 8), :] * keep_y[1]
            high = pl.ds(8 + level.n, 8)
            ref[x, high, :] = ref[x, high, :] * keep_y[-1]
            return carry

        lax.fori_loop(0, level.n + 2 * w, edges, 0)

    zero_outside(mid, km, mid_k)
    for copy in mid_a:
        copy.wait_recv()
    setup(mid, at(km, mid.ny), at(am, mid.ny), wm)
    zero_outside(coarse, kc, coarse_k)
    for copy in coarse_a:
        copy.wait_recv()
    setup(coarse, at(kc, coarse.ny), at(ac, coarse.ny), wc)
    for copy in mid_s:
        copy.wait_recv()
    start_iterate(mid, of(sm), wm[4], um[0])

    def mid_finish(x, new, total, c, inv):
        midi[x] = total
        midr[x] = jnp.where(inv > 0.0, new, 0.0)

    sweeps(mid, of(sm), wm, rm, um, mid_finish)

    pool(lambda x, y: midr[x, pl.ds(y, coarse.n, stride=2), :],
         writer(sc, coarse.margin, coarse.n), coarse.n, mid.stride)
    coarse_s = halo(sc, sc, coarse.n, coarse.margin, coarse.margin, (coarse.margin, 8))

    def pick(value, stride):
        cells = LANES // stride
        chosen = (lax.broadcasted_iota(jnp.int32, (LANES, cells), 0)
                  == stride * lax.broadcasted_iota(jnp.int32, (LANES, cells), 1)).astype(F32)
        return jnp.dot(value, chosen, preferred_element_type=F32, precision=lax.Precision.HIGHEST)

    mid_out[...] = pick(midi[...].reshape(mid.n * mid.n, LANES), mid.stride).reshape(mid_out.shape)
    for copy in coarse_s:
        copy.wait_recv()
    start_iterate(coarse, of(sc), wc[4], uc[0])
    a, b = coarse.steps[-1]

    def coarse_finish(x, new, total, c, inv):
        coai[x] = total + (a * c + b * (inv * new))

    sweeps(coarse, of(sc), wc, rc, uc, coarse_finish)
    coarse_out[...] = pick(coai[...].reshape(coarse.n * coarse.n, LANES),
                           coarse.stride).reshape(coarse_out.shape)

    for group in (bricks, fine_k, fine_a, fine_s, mid_k, mid_a, coarse_k, coarse_a, mid_s, coarse_s):
        for copy in group:
            copy.wait_send()


def step(source, conductivity, absorption, brick_mask):
    n = source.shape[0]
    fine = Level(n, DEGREE, n + 2 * DEGREE, 1, STEP_SCALE, DEGREE, SMOOTH_LOW)
    mid = Level(n // 2, DEGREE, n // 2 + 2 * DEGREE, 2, STEP_SCALE / 4.0, DEGREE, SMOOTH_LOW)
    coarse = Level(n // 4, COARSE_DEGREE - 1, 24, 4, STEP_SCALE / 16.0, COARSE_DEGREE, COARSE_LOW)
    levels = (fine, mid, coarse)

    def kernel(*refs):
        body_kernel(levels, *refs)

    fields = []
    for level in levels:
        fields += [pltpu.VMEM(level.coefficient_shape(), F32), pltpu.VMEM(level.source_shape(), F32),
                   pltpu.VMEM(level.source_shape(), F32)]
    order = [fields[0], fields[1], fields[2], fields[3], fields[4], fields[5], fields[6], fields[7], fields[8]]
    copies = 10 * len(DIRS)
    scratch = order + [
        pltpu.VMEM((len(DIRS),) + brick_mask.shape, jnp.int32),
        pltpu.VMEM((48, 16), F32),
        pltpu.VMEM((48, LANES), F32),
        pltpu.VMEM((mid.n, mid.n, LANES), F32),
        pltpu.VMEM((mid.n, mid.n, LANES), F32),
        pltpu.VMEM((coarse.n, coarse.n, LANES), F32),
    ]
    scratch += [[pltpu.VMEM(level.work_shape(), F32)] * 5 for level in levels]
    scratch += [pltpu.VMEM(level.work_shape(), F32) for level in levels]
    scratch += [[pltpu.VMEM(level.work_shape(), F32)] * count
                for level, count in zip(levels, (DEGREE, DEGREE, COARSE_DEGREE - 1))]
    scratch += [pltpu.SemaphoreType.DMA((3,)), pltpu.SemaphoreType.DMA((copies,)),
                pltpu.SemaphoreType.DMA((copies,))]
    vmem = pl.BlockSpec(memory_space=pltpu.VMEM)
    anywhere = pl.BlockSpec(memory_space=pl.ANY)
    return pl.pallas_call(
        kernel,
        out_shape=(
            jax.ShapeDtypeStruct((n, n, LANES), F32),
            jax.ShapeDtypeStruct((n, n, LANES), F32),
            jax.ShapeDtypeStruct((mid.n, mid.n, LANES // 2), F32),
            jax.ShapeDtypeStruct((coarse.n, coarse.n, LANES // 4), F32),
        ),
        in_specs=[anywhere, anywhere, anywhere, vmem],
        out_specs=(vmem, vmem, vmem, vmem),
        scratch_shapes=scratch,
        compiler_params=pltpu.CompilerParams(collective_id=0, has_side_effects=True,
                                             vmem_limit_bytes=56 * 1024 * 1024),
    )(source, conductivity, absorption, brick_mask)


def solution(mesh):
    spec = P("dom", "grp", None)
    return jax.shard_map(step, mesh=mesh, in_specs=(spec,) * 4, out_specs=(spec,) * 4, check_vma=False)
```

time: 297 us -> 70.9 us (0.24)
  the two profiles are of different devices: /device:TPU:25 before, /device:TPU:1 now
where the time goes in v1:
time: 70.9 us; the launch traced here: 70.6 us
  Pallas kernels  65.7 us (93%)
  local copies, waits for them, and re-layouts  4.32 us (6%)
    pallas_call x1, Pallas kernels, step(): pl.pallas_call(kernel, out_shape=(jax.ShapeDtypeStruct((n, n, LANES), F32...  65.7 us
    unnamed x10, local copies, waits for them, and re-layouts  4.32 us

profile of v1, /device:TPU:1, one launch (start us, length us, event | category | flops | bytes accessed | tf_op | source)
XLA Modules:
  0.0 70.6 jit_solution(12928364245287509320)
XLA Ops:
  0.6 65.7 %shard_map.75 = (f32[32,32,128]{2,1,0:T(8,128)}, f32[32,32,128]{2,1,0:T(8,128)}, f32[16,16,64]{2,1,0:T(8,128)}, f32[8,8,32]{2,1,0:T(8,128)}) custom-call(f32[32,32,128]{2,1,0:T(8,128)} %refs_0_.1, f32[32,32,128]{2,1,0:T(8,128)} %refs_1_.1, f32[32,32,128]{2,1,0:T(8,128)} %refs_2_.1, s32[4,4,16]{2,1,0:T(4,128)} %refs_3_.1), custom_call_target="tpu_custom_call" | custom-call | tf_op jit(solution)/shard_map/pallas_call | solution.py:418
  66.3 0.0 copy-start
  66.3 1.9 %copy.12 = f32[32,32,128]{2,1,0:T(8,128)} copy(f32[32,32,128]{2,1,0:T(8,128)} %get-tuple-element.8) | data formatting | bytes 1048576
  68.2 0.0 copy-done
  68.2 0.0 copy-start.1
  68.3 0.8 %copy.13 = f32[32,32,128]{2,1,0:T(8,128)} copy(f32[32,32,128]{2,1,0:T(8,128)S(1)} %copy-done) | data formatting | bytes 1048576
  69.0 0.2 copy-done.1
  69.3 0.0 copy-start.2
  69.3 0.7 copy.14
  69.9 0.1 copy-done.2
  70.0 0.6 copy.15
Async XLA Ops:
  66.3 1.9 %copy-start = (f32[32,32,128]{2,1,0:T(8,128)S(1)}, f32[32,32,128]{2,1,0:T(8,128)}, u32[]{:S(2)}) copy-start(f32[32,32,128]{2,1,0:T(8,128)} %get-tuple-element.9) | copy-start | bytes 1572868
  68.2 1.0 %copy-start.1 = (f32[16,16,64]{2,1,0:T(8,128)S(1)}, f32[16,16,64]{2,1,0:T(8,128)}, u32[]{:S(2)}) copy-start(f32[16,16,64]{2,1,0:T(8,128)} %get-tuple-element.10) | copy-start | bytes 196612
  69.3 0.8 %copy-start.2 = (f32[8,8,32]{2,1,0:T(8,128)S(1)}, f32[8,8,32]{2,1,0:T(8,128)}, u32[]{:S(2)}) copy-start(f32[8,8,32]{2,1,0:T(8,128)} %get-tuple-element.11) | copy-start | bytes 24580

commit v2 on v1

v2 whole, which is shorter than its diff:
```python
import jax
import jax.numpy as jnp
from jax import lax
from jax.experimental import pallas as pl
from jax.experimental.pallas import tpu as pltpu
from jax.sharding import PartitionSpec as P

DEGREE = 4
COARSE_DEGREE = 6
STEP_SCALE = 4.0
SMOOTH_LOW = 0.3
SMOOTH_HIGH = 2.0
COARSE_LOW = 0.05
LANES = 128
MESH = pl.DeviceIdType.MESH
DIRS = ((1, 0), (1, 1), (1, -1), (0, 1), (0, -1), (-1, 0), (-1, 1), (-1, -1))
BLOCK = 4
F32 = jnp.float32


def recurrence(degree, lowest, highest):
    middle = (highest + lowest) / 2.0
    spread = (highest - lowest) / 2.0
    relative = middle / spread
    factor = 1.0 / relative
    steps = []
    for _ in range(degree - 1):
        following = 1.0 / (2.0 * relative - factor)
        steps.append((following * factor, 2.0 * following / spread))
        factor = following
    return 1.0 / middle, tuple(steps)


class Level:
    def __init__(self, n, margin, rows, stride, scale, degree, lowest):
        self.n, self.margin, self.stride, self.scale = n, margin, stride, scale
        self.nx = n + 2 * margin
        self.y0 = 8 - margin
        self.ny = rows
        self.yb = 8 * ((self.y0 + rows + 1 + 7) // 8)
        self.first, self.steps = recurrence(degree, lowest, SMOOTH_HIGH)
        self.degree = degree

    def coefficient_shape(self):
        return (self.n + 2 * self.margin + 2, self.yb, LANES)

    def source_shape(self):
        return (self.nx, self.yb, LANES)

    def work_shape(self):
        return (self.nx, self.ny + 16, LANES)


def span(sign, n, margin):
    if sign == 0:
        return 0, n
    return (n - margin, margin) if sign > 0 else (0, margin)


def landing(sign, n, margin, offset):
    if sign == 0:
        return offset
    return offset - margin if sign > 0 else offset + n


def lane_index():
    return lax.broadcasted_iota(jnp.int32, (1, LANES), 1)


def blocks(low, high, body):
    steps, rest = divmod(high - low, BLOCK)

    def turn(s, carry):
        body(low + s * BLOCK, BLOCK)
        return carry

    if steps:
        lax.fori_loop(0, steps, turn, 0)
    if rest:
        body(high - rest, rest)


def pool(read, write, count, stride):
    even = lax.rem(lane_index() // stride, 2) == 0

    def body(first, rows):
        for i in range(rows):
            x = 2 * (first + i)
            p = (read(x, 0) + read(x, 1)) + (read(x + 1, 0) + read(x + 1, 1))
            other = jnp.where(even, pltpu.roll(p, LANES - stride, 1), pltpu.roll(p, stride, 1))
            write(first + i, (p + other) * 0.125)

    blocks(0, count, body)


def setup(level, kappa, absorb, work, source=None, u0=None):
    wx, wy, wz, diag, inv = work
    half = level.scale * 0.5
    up = lane_index() < LANES - level.stride
    down = lane_index() >= level.stride
    y0, ny = level.y0, level.ny

    def flag(k):
        return jnp.where(k > 0.0, 1.0, 0.0)

    def body(first, rows):
        ks = [kappa(first + x, y0) for x in range(rows + 2)]
        flags = [flag(k) for k in ks]
        for r in range(rows):
            i = first + r
            k, xp, xm = ks[r + 1], ks[r + 2], ks[r]
            yp, ym = kappa(i + 1, y0 + 1), kappa(i + 1, y0 - 1)
            zp = jnp.where(up, pltpu.roll(k, LANES - level.stride, 1), 0.0)
            zm = jnp.where(down, pltpu.roll(k, level.stride, 1), 0.0)
            total = (xp + xm) + (yp + ym) + (zp + zm)
            count = (flags[r + 2] + flags[r]) + (flag(yp) + flag(ym)) + (flag(zp) + flag(zm))
            d = (1.0 + half * (k * count + total)) + level.scale * absorb(i, y0) * (6.0 - count)
            at = pl.ds(8, ny)
            wx[i, at, :] = half * (k + xp)
            wy[i, at, :] = half * (k + yp)
            wz[i, at, :] = jnp.where(up, half * (k + zp), 0.0)
            diag[i, at, :] = d
            v = flags[r + 1] / d
            inv[i, at, :] = v
            if u0 is not None:
                u0[i, at, :] = (v * source(i, y0, ny)) * level.first

    blocks(0, level.nx, body)


def start_iterate(level, source, inv, u0):
    at = pl.ds(8, level.ny)

    def body(first, rows):
        for i in range(rows):
            u0[first + i, at, :] = (inv[first + i, at, :] * source(first + i, level.y0, level.ny)) * level.first

    blocks(0, level.nx, body)


def residual_rows(level, work, u, old, first, rows, start, size):
    wx, wy, wz, diag, inv = work
    at, above, below = pl.ds(start, size), pl.ds(start + 1, size), pl.ds(start - 1, size)
    us = [u[first + x - 1, at, :] for x in range(rows + 2)]
    ws = [wx[first + x - 1, at, :] for x in range(rows + 1)]
    out = []
    for r in range(rows):
        i, c = first + r, us[r + 1]
        t = ws[r + 1] * us[r + 2] + ws[r] * us[r]
        t = t + (wy[i, at, :] * u[i, above, :] + wy[i, below, :] * u[i, below, :])
        z = wz[i, at, :]
        t = t + (z * pltpu.roll(c, LANES - level.stride, 1) + pltpu.roll(z * c, level.stride, 1))
        out.append(((old(i) - diag[i, at, :] * c) + t, c))
    return out


def sweeps(level, source, work, r, us, finish):
    inv = work[4]
    last = len(us) - 1
    m, n = level.margin, level.n
    at = pl.ds(8, level.ny)
    for k in range(last):
        a, b = level.steps[k]

        def body(first, rows, k=k, a=a, b=b):
            def old(i):
                return source(i, level.y0, level.ny) if k == 0 else r[i, at, :]

            for x, (new, c) in enumerate(
                    residual_rows(level, work, us[k], old, first, rows, 8, level.ny)):
                r[first + x, at, :] = new
                us[k + 1][first + x, at, :] = a * c + b * (inv[first + x, at, :] * new)

        blocks(k + 1, level.nx - 1 - k, body)

    own = pl.ds(8 + m, n)

    def body(first, rows):
        for x, (new, c) in enumerate(
                residual_rows(level, work, us[last], lambda i: r[i, own, :], first, rows, 8 + m, n)):
            total = us[0][first + x, own, :]
            for u in us[1:-1]:
                total = total + u[first + x, own, :]
            finish(first + x - m, new, total + c, c, inv[first + x, own, :])

    blocks(m, m + n, body)


def body_kernel(levels, s_in, k_in, a_in, b_in, it_out, res_out, mid_out, coarse_out,
                kf, sf, af, km, am, sm, kc, ac, sc, fm, midr, midi, coai,
                wf, wm, wc, rf, rm, rc, uf, um, uc, local, send, recv):
    fine, mid, coarse = levels
    d, g = lax.axis_index("dom"), lax.axis_index("grp")
    nd, ng = lax.axis_size("dom"), lax.axis_size("grp")
    low_x, high_x = d > 0, d < nd - 1
    low_y, high_y = g > 0, g < ng - 1

    def both(p, q):
        return q if p is None else p if q is None else jnp.logical_and(p, q)

    def target(dx, dg):
        return both({0: None, 1: high_x, -1: low_x}[dx], {0: None, 1: high_y, -1: low_y}[dg])

    def neighbour(dx, dg):
        return (lax.rem(d + (nd + dx), nd), lax.rem(g + (ng + dg), ng))

    barrier = pltpu.get_barrier_semaphore()
    for dx, dg in DIRS:
        @pl.when(target(dx, dg))
        def _(dx=dx, dg=dg):
            pl.semaphore_signal(barrier, inc=1, device_id=neighbour(dx, dg), device_id_type=MESH)

    loads = []
    for slot, (operand, buffer, off) in enumerate(
            ((k_in, kf, fine.margin + 1), (a_in, af, fine.margin), (s_in, sf, fine.margin))):
        copy = pltpu.make_async_copy(operand, buffer.at[pl.ds(off, fine.n), pl.ds(8, fine.n), :],
                                     local.at[slot])
        copy.start()
        loads.append(copy)

    fields = ((kf, fine, 1), (af, fine, 0), (sf, fine, 0), (km, mid, 1), (am, mid, 0), (sm, mid, 0),
              (kc, coarse, 1), (ac, coarse, 0), (sc, coarse, 0))
    for ref, level, extra in fields:
        w = level.margin + extra
        rows, cells = level.n + 2 * w, level.n
        for missing, x0 in ((d == 0, 0), (d == nd - 1, w + cells)):
            @pl.when(missing)
            def _(ref=ref, level=level, w=w, x0=x0):
                for x in range(w):
                    ref[x0 + x] = jnp.zeros((level.yb, LANES), F32)
        for missing, y0 in ((g == 0, 0), (g == ng - 1, 8 + cells)):
            @pl.when(missing)
            def _(ref=ref, rows=rows, y0=y0):
                def clear(x, carry):
                    ref[x, pl.ds(y0, 8), :] = jnp.zeros((8, LANES), F32)
                    return carry
                lax.fori_loop(0, rows, clear, 0)

    lanes_of = (lax.broadcasted_iota(jnp.int32, (16, LANES), 1) // 8
                == lax.broadcasted_iota(jnp.int32, (16, LANES), 0)).astype(F32)
    for bx in range(4):
        fm[pl.ds(8 * bx, 4), :] = jnp.dot(b_in[bx].astype(F32), lanes_of, preferred_element_type=F32)

    loads[0].wait()
    kx = fine.margin + 1

    def mask_own(s, carry):
        for t in range(4):
            flag = jnp.broadcast_to(fm[pl.ds(8 * (s // 2) + t, 1), :], (8, LANES))
            for x in range(4):
                at = (kx + 4 * s + x, pl.ds(8 + 8 * t, 8), slice(None))
                kf[at] = kf[at] * flag
        return carry

    lax.fori_loop(0, fine.n // 4, mask_own, 0)
    loads[1].wait()
    loads[2].wait()
    count_x = low_x.astype(jnp.int32) + high_x.astype(jnp.int32) + 1
    count_y = low_y.astype(jnp.int32) + high_y.astype(jnp.int32) + 1
    pl.semaphore_wait(barrier, count_x * count_y - 1)

    used = [0]
    groups = []

    def halo(parts):
        group = []
        for dx, dg in DIRS:
            copies = []
            for ref, level, width in parts:
                n = level.n
                sx, cx = span(dx, n, width)
                sy, cy = span(dg, n, width)
                slot = used[0]
                used[0] += 1
                copies.append(pltpu.make_async_remote_copy(
                    src_ref=ref.at[pl.ds(width + sx, cx), pl.ds(8 + sy, cy), :],
                    dst_ref=ref.at[pl.ds(landing(dx, n, width, width), cx),
                                   pl.ds(landing(dg, n, width, 8), cy), :],
                    send_sem=send.at[slot], recv_sem=recv.at[slot],
                    device_id=neighbour(dx, dg), device_id_type=MESH))

            @pl.when(target(dx, dg))
            def _(copies=copies):
                for copy in copies:
                    copy.start()

            group.append((dx, dg, copies))
        groups.append(group)
        return group

    def arrive(group):
        for dx, dg, copies in group:
            @pl.when(target(-dx, -dg))
            def _(copies=copies):
                for copy in copies:
                    copy.wait_recv()

    mx, cx = mid.margin + 1, coarse.margin + 1
    fine_halo = halo(((kf, fine, kx), (af, fine, fine.margin), (sf, fine, fine.margin)))

    def reader(ref, x0, count):
        return lambda x, y: ref[x + x0, pl.ds(8 + y, count, stride=2), :]

    def writer(ref, x0, count):
        def write(x, value):
            ref[x + x0, pl.ds(8, count), :] = value
        return write

    pool(reader(kf, kx, mid.n), writer(km, mx, mid.n), mid.n, fine.stride)
    pool(reader(af, fine.margin, mid.n), writer(am, mid.margin, mid.n), mid.n, fine.stride)
    pool(reader(km, mx, coarse.n), writer(kc, cx, coarse.n), coarse.n, mid.stride)
    pool(reader(am, mid.margin, coarse.n), writer(ac, coarse.margin, coarse.n), coarse.n, mid.stride)
    side_halo = halo(((km, mid, mx), (am, mid, mid.margin), (kc, coarse, cx), (ac, coarse, coarse.margin)))

    def at(ref, size):
        return lambda x, y: ref[x, pl.ds(y, size), :]

    def of(ref):
        return lambda x, y, size: ref[x, pl.ds(y, size), :]

    arrive(fine_halo)
    setup(fine, at(kf, fine.ny), at(af, fine.ny), wf, of(sf), uf[0])

    def fine_finish(x, new, total, c, inv):
        it_out[x] = total
        res_out[x] = jnp.where(inv > 0.0, new, 0.0)

    sweeps(fine, of(sf), wf, rf, uf, fine_finish)

    pool(lambda x, y: res_out[x, pl.ds(y, mid.n, stride=2), :], writer(sm, mid.margin, mid.n),
         mid.n, fine.stride)
    mid_halo = halo(((sm, mid, mid.margin),))
    arrive(side_halo)
    setup(mid, at(km, mid.ny), at(am, mid.ny), wm)
    setup(coarse, at(kc, coarse.ny), at(ac, coarse.ny), wc)
    arrive(mid_halo)
    start_iterate(mid, of(sm), wm[4], um[0])

    def mid_finish(x, new, total, c, inv):
        midi[x] = total
        midr[x] = jnp.where(inv > 0.0, new, 0.0)

    sweeps(mid, of(sm), wm, rm, um, mid_finish)

    pool(lambda x, y: midr[x, pl.ds(y, coarse.n, stride=2), :],
         writer(sc, coarse.margin, coarse.n), coarse.n, mid.stride)
    coarse_halo = halo(((sc, coarse, coarse.margin),))

    def pick(value, stride):
        cells = LANES // stride
        chosen = (lax.broadcasted_iota(jnp.int32, (LANES, cells), 0)
                  == stride * lax.broadcasted_iota(jnp.int32, (LANES, cells), 1)).astype(F32)
        return jnp.dot(value, chosen, preferred_element_type=F32, precision=lax.Precision.HIGHEST)

    mid_out[...] = pick(midi[...].reshape(mid.n * mid.n, LANES), mid.stride).reshape(mid_out.shape)
    arrive(coarse_halo)
    start_iterate(coarse, of(sc), wc[4], uc[0])
    a, b = coarse.steps[-1]

    def coarse_finish(x, new, total, c, inv):
        coai[x] = total + (a * c + b * (inv * new))

    sweeps(coarse, of(sc), wc, rc, uc, coarse_finish)
    coarse_out[...] = pick(coai[...].reshape(coarse.n * coarse.n, LANES),
                           coarse.stride).reshape(coarse_out.shape)

    for position in range(len(DIRS)):
        dx, dg = DIRS[position]

        @pl.when(target(dx, dg))
        def _(position=position):
            for group in groups:
                for copy in group[position][2]:
                    copy.wait_send()


def step(source, conductivity, absorption, brick_mask):
    n = source.shape[0]
    fine = Level(n, DEGREE, n + 2 * DEGREE, 1, STEP_SCALE, DEGREE, SMOOTH_LOW)
    mid = Level(n // 2, DEGREE, n // 2 + 2 * DEGREE, 2, STEP_SCALE / 4.0, DEGREE, SMOOTH_LOW)
    coarse = Level(n // 4, COARSE_DEGREE - 1, 24, 4, STEP_SCALE / 16.0, COARSE_DEGREE, COARSE_LOW)
    levels = (fine, mid, coarse)

    def kernel(*refs):
        body_kernel(levels, *refs)

    fields = []
    for level in levels:
        fields += [pltpu.VMEM(level.coefficient_shape(), F32), pltpu.VMEM(level.source_shape(), F32),
                   pltpu.VMEM(level.source_shape(), F32)]
    copies = 9 * len(DIRS)
    scratch = fields + [
        pltpu.VMEM((32, LANES), F32),
        pltpu.VMEM((mid.n, mid.n, LANES), F32),
        pltpu.VMEM((mid.n, mid.n, LANES), F32),
        pltpu.VMEM((coarse.n, coarse.n, LANES), F32),
    ]
    scratch += [[pltpu.VMEM(level.work_shape(), F32)] * 5 for level in levels]
    scratch += [pltpu.VMEM(level.work_shape(), F32) for level in levels]
    scratch += [[pltpu.VMEM(level.work_shape(), F32)] * count
                for level, count in zip(levels, (DEGREE, DEGREE, COARSE_DEGREE - 1))]
    scratch += [pltpu.SemaphoreType.DMA((3,)), pltpu.SemaphoreType.DMA((copies,)),
                pltpu.SemaphoreType.DMA((copies,))]
    vmem = pl.BlockSpec(memory_space=pltpu.VMEM)
    anywhere = pl.BlockSpec(memory_space=pl.ANY)
    return pl.pallas_call(
        kernel,
        out_shape=(
            jax.ShapeDtypeStruct((n, n, LANES), F32),
            jax.ShapeDtypeStruct((n, n, LANES), F32),
            jax.ShapeDtypeStruct((mid.n, mid.n, LANES // 2), F32),
            jax.ShapeDtypeStruct((coarse.n, coarse.n, LANES // 4), F32),
        ),
        in_specs=[anywhere, anywhere, anywhere, vmem],
        out_specs=(vmem, vmem, vmem, vmem),
        scratch_shapes=scratch,
        compiler_params=pltpu.CompilerParams(collective_id=0, has_side_effects=True,
                                             vmem_limit_bytes=56 * 1024 * 1024),
    )(source, conductivity, absorption, brick_mask)


def solution(mesh):
    spec = P("dom", "grp", None)
    return jax.shard_map(step, mesh=mesh, in_specs=(spec,) * 4, out_specs=(spec,) * 4, check_vma=False)
```

time: 70.9 us -> 47.2 us (0.67)
  the two profiles are of different devices: /device:TPU:1 before, /device:TPU:25 now
where the time goes in v2:
time: 47.2 us; the launch traced here: 46.9 us
  Pallas kernels  42 us (89%)
  local copies, waits for them, and re-layouts  4.32 us (9%)
  between operations  0.65 us (1%)
    pallas_call x1, Pallas kernels, step(): pl.pallas_call(kernel, out_shape=(jax.ShapeDtypeStruct((n, n, LANES), F32...  42 us
    unnamed x10, local copies, waits for them, and re-layouts  4.32 us

profile of v2, /device:TPU:25, one launch (start us, length us, event | category | flops | bytes accessed | tf_op | source)
XLA Modules:
  0.0 46.9 jit_solution(11885597087090855915)
XLA Ops:
  0.6 42.0 %shard_map.75 = (f32[32,32,128]{2,1,0:T(8,128)}, f32[32,32,128]{2,1,0:T(8,128)}, f32[16,16,64]{2,1,0:T(8,128)}, f32[8,8,32]{2,1,0:T(8,128)}) custom-call(f32[32,32,128]{2,1,0:T(8,128)} %refs_0_.1, f32[32,32,128]{2,1,0:T(8,128)} %refs_1_.1, f32[32,32,128]{2,1,0:T(8,128)} %refs_2_.1, s32[4,4,16]{2,1,0:T(4,128)} %refs_3_.1), custom_call_target="tpu_custom_call" | custom-call | tf_op jit(solution)/shard_map/pallas_call | solution.py:406
  42.6 0.0 copy-start
  42.6 1.9 %copy.12 = f32[32,32,128]{2,1,0:T(8,128)} copy(f32[32,32,128]{2,1,0:T(8,128)} %get-tuple-element.8) | data formatting | bytes 1048576
  44.5 0.0 copy-done
  44.5 0.0 copy-start.1
  44.6 0.8 %copy.13 = f32[32,32,128]{2,1,0:T(8,128)} copy(f32[32,32,128]{2,1,0:T(8,128)S(1)} %copy-done) | data formatting | bytes 1048576
  45.3 0.2 copy-done.1
  45.6 0.0 copy-start.2
  45.6 0.7 %copy.14 = f32[16,16,64]{2,1,0:T(8,128)} copy(f32[16,16,64]{2,1,0:T(8,128)S(1)} %copy-done.1) | data formatting | bytes 131072
  46.2 0.1 copy-done.2
  46.3 0.6 %copy.15 = f32[8,8,32]{2,1,0:T(8,128)} copy(f32[8,8,32]{2,1,0:T(8,128)S(1)} %copy-done.2) | data formatting | bytes 16384
Async XLA Ops:
  42.6 1.9 %copy-start = (f32[32,32,128]{2,1,0:T(8,128)S(1)}, f32[32,32,128]{2,1,0:T(8,128)}, u32[]{:S(2)}) copy-start(f32[32,32,128]{2,1,0:T(8,128)} %get-tuple-element.9) | copy-start | bytes 1572868
  44.5 1.0 %copy-start.1 = (f32[16,16,64]{2,1,0:T(8,128)S(1)}, f32[16,16,64]{2,1,0:T(8,128)}, u32[]{:S(2)}) copy-start(f32[16,16,64]{2,1,0:T(8,128)} %get-tuple-element.10) | copy-start | bytes 196612
  45.6 0.8 %copy-start.2 = (f32[8,8,32]{2,1,0:T(8,128)S(1)}, f32[8,8,32]{2,1,0:T(8,128)}, u32[]{:S(2)}) copy-start(f32[8,8,32]{2,1,0:T(8,128)} %get-tuple-element.11) | copy-start | bytes 24580

commit v3 on v2

--- a/solution.py
+++ b/solution.py
@@ -13,8 +13,9 @@
 COARSE_LOW = 0.05
 LANES = 128
 MESH = pl.DeviceIdType.MESH
-DIRS = ((1, 0), (1, 1), (1, -1), (0, 1), (0, -1), (-1, 0), (-1, 1), (-1, -1))
-BLOCK = 4
+DIRS = ((0, 1), (0, -1), (1, 0), (1, 1), (1, -1), (-1, 0), (-1, 1), (-1, -1))
+BLOCK = 14
+FAR_FIRST = ((1, 1), (1, -1), (-1, 1), (-1, -1), (1, 0), (-1, 0), (0, 1), (0, -1))
 F32 = jnp.float32
 
 
@@ -39,7 +40,7 @@
         self.ny = rows
         self.yb = 8 * ((self.y0 + rows + 1 + 7) // 8)
         self.first, self.steps = recurrence(degree, lowest, SMOOTH_HIGH)
-        self.degree = degree
+        self.block = BLOCK if rows > 24 else 24
 
     def coefficient_shape(self):
         return (self.n + 2 * self.margin + 2, self.yb, LANES)
@@ -67,14 +68,16 @@
     return lax.broadcasted_iota(jnp.int32, (1, LANES), 1)
 
 
-def blocks(low, high, body):
-    steps, rest = divmod(high - low, BLOCK)
+def blocks(low, high, body, most=BLOCK):
+    steps, rest = divmod(high - low, most)
 
     def turn(s, carry):
-        body(low + s * BLOCK, BLOCK)
+        body(low + s * most, most)
         return carry
 
-    if steps:
+    if steps == 1:
+        body(low, most)
+    elif steps:
         lax.fori_loop(0, steps, turn, 0)
     if rest:
         body(high - rest, rest)
@@ -93,7 +96,7 @@
     blocks(0, count, body)
 
 
-def setup(level, kappa, absorb, work, source=None, u0=None):
+def setup(level, kappa, absorb, work, source=None, u0=None, span_x=None):
     wx, wy, wz, diag, inv = work
     half = level.scale * 0.5
     up = lane_index() < LANES - level.stride
@@ -125,7 +128,7 @@
             if u0 is not None:
                 u0[i, at, :] = (v * source(i, y0, ny)) * level.first
 
-    blocks(0, level.nx, body)
+    blocks(*(span_x or (0, level.nx)), body, level.block)
 
 
 def start_iterate(level, source, inv, u0):
@@ -135,7 +138,7 @@
         for i in range(rows):
             u0[first + i, at, :] = (inv[first + i, at, :] * source(first + i, level.y0, level.ny)) * level.first
 
-    blocks(0, level.nx, body)
+    blocks(0, level.nx, body, level.block)
 
 
 def residual_rows(level, work, u, old, first, rows, start, size):
@@ -154,11 +157,12 @@
     return out
 
 
-def sweeps(level, source, work, r, us, finish):
+def sweeps(level, source, work, r, us, finish, span_of=None):
     inv = work[4]
     last = len(us) - 1
     m, n = level.margin, level.n
     at = pl.ds(8, level.ny)
+    span_of = span_of or (lambda k: (k + 1, level.nx - 1 - k))
     for k in range(last):
         a, b = level.steps[k]
 
@@ -171,7 +175,7 @@
                 r[first + x, at, :] = new
                 us[k + 1][first + x, at, :] = a * c + b * (inv[first + x, at, :] * new)
 
-        blocks(k + 1, level.nx - 1 - k, body)
+        blocks(*span_of(k), body, level.block)
 
     own = pl.ds(8 + m, n)
 
@@ -183,7 +187,7 @@
                 total = total + u[first + x, own, :]
             finish(first + x - m, new, total + c, c, inv[first + x, own, :])
 
-    blocks(m, m + n, body)
+    blocks(*span_of(last), body, level.block)
 
 
 def body_kernel(levels, s_in, k_in, a_in, b_in, it_out, res_out, mid_out, coarse_out,
@@ -241,6 +245,9 @@
     for bx in range(4):
         fm[pl.ds(8 * bx, 4), :] = jnp.dot(b_in[bx].astype(F32), lanes_of, preferred_element_type=F32)
 
+    count_x = low_x.astype(jnp.int32) + high_x.astype(jnp.int32) + 1
+    count_y = low_y.astype(jnp.int32) + high_y.astype(jnp.int32) + 1
+
     loads[0].wait()
     kx = fine.margin + 1
 
@@ -255,16 +262,15 @@
     lax.fori_loop(0, fine.n // 4, mask_own, 0)
     loads[1].wait()
     loads[2].wait()
-    count_x = low_x.astype(jnp.int32) + high_x.astype(jnp.int32) + 1
-    count_y = low_y.astype(jnp.int32) + high_y.astype(jnp.int32) + 1
+
     pl.semaphore_wait(barrier, count_x * count_y - 1)
 
     used = [0]
     groups = []
 
-    def halo(parts):
-        group = []
-        for dx, dg in DIRS:
+    def halo(parts, order):
+        group = {}
+        for dx, dg in order:
             copies = []
             for ref, level, width in parts:
                 n = level.n
@@ -284,19 +290,22 @@
                 for copy in copies:
                     copy.start()
 
-            group.append((dx, dg, copies))
+            group[dx, dg] = copies
         groups.append(group)
         return group
 
-    def arrive(group):
-        for dx, dg, copies in group:
+    def arrive(group, signs=(-1, 0, 1)):
+        for (dx, dg), copies in group.items():
+            if dx not in signs:
+                continue
+
             @pl.when(target(-dx, -dg))
             def _(copies=copies):
                 for copy in copies:
                     copy.wait_recv()
 
     mx, cx = mid.margin + 1, coarse.margin + 1
-    fine_halo = halo(((kf, fine, kx), (af, fine, fine.margin), (sf, fine, fine.margin)))
+    fine_halo = halo(((kf, fine, kx), (af, fine, fine.margin), (sf, fine, fine.margin)), DIRS)
 
     def reader(ref, x0, count):
         return lambda x, y: ref[x + x0, pl.ds(8 + y, count, stride=2), :]
@@ -310,26 +319,35 @@
     pool(reader(af, fine.margin, mid.n), writer(am, mid.margin, mid.n), mid.n, fine.stride)
     pool(reader(km, mx, coarse.n), writer(kc, cx, coarse.n), coarse.n, mid.stride)
     pool(reader(am, mid.margin, coarse.n), writer(ac, coarse.margin, coarse.n), coarse.n, mid.stride)
-    side_halo = halo(((km, mid, mx), (am, mid, mid.margin), (kc, coarse, cx), (ac, coarse, coarse.margin)))
+    side_halo = halo(((km, mid, mx), (am, mid, mid.margin), (kc, coarse, cx), (ac, coarse, coarse.margin)),
+                     DIRS)
 
     def at(ref, size):
         return lambda x, y: ref[x, pl.ds(y, size), :]
 
     def of(ref):
         return lambda x, y, size: ref[x, pl.ds(y, size), :]
-
-    arrive(fine_halo)
-    setup(fine, at(kf, fine.ny), at(af, fine.ny), wf, of(sf), uf[0])
 
     def fine_finish(x, new, total, c, inv):
         it_out[x] = total
         res_out[x] = jnp.where(inv > 0.0, new, 0.0)
 
-    sweeps(fine, of(sf), wf, rf, uf, fine_finish)
+    def fine_part(low, high, span_of):
+        setup(fine, at(kf, fine.ny), at(af, fine.ny), wf, of(sf), uf[0], (low, high))
+        sweeps(fine, of(sf), wf, rf, uf, fine_finish, span_of)
+
+    edge, end = fine.margin + 1, fine.nx - fine.margin - 1
+    arrive(fine_halo, (0,))
+    fine_part(edge, end, lambda k: (edge + 1 + k, end - 1 - k))
+    arrive(fine_halo, (-1,))
+    fine_part(end, fine.nx, lambda k: (end - 1 - k, fine.nx - 1 - k))
+
+    arrive(fine_halo, (1,))
+    fine_part(0, edge, lambda k: (k + 1, edge + 1 + k))
 
     pool(lambda x, y: res_out[x, pl.ds(y, mid.n, stride=2), :], writer(sm, mid.margin, mid.n),
          mid.n, fine.stride)
-    mid_halo = halo(((sm, mid, mid.margin),))
+    mid_halo = halo(((sm, mid, mid.margin),), FAR_FIRST)
     arrive(side_halo)
     setup(mid, at(km, mid.ny), at(am, mid.ny), wm)
     setup(coarse, at(kc, coarse.ny), at(ac, coarse.ny), wc)
@@ -344,7 +362,7 @@
 
     pool(lambda x, y: midr[x, pl.ds(y, coarse.n, stride=2), :],
          writer(sc, coarse.margin, coarse.n), coarse.n, mid.stride)
-    coarse_halo = halo(((sc, coarse, coarse.margin),))
+    coarse_halo = halo(((sc, coarse, coarse.margin),), FAR_FIRST)
 
     def pick(value, stride):
         cells = LANES // stride
@@ -364,13 +382,11 @@
     coarse_out[...] = pick(coai[...].reshape(coarse.n * coarse.n, LANES),
                            coarse.stride).reshape(coarse_out.shape)
 
-    for position in range(len(DIRS)):
-        dx, dg = DIRS[position]
-
+    for dx, dg in DIRS:
         @pl.when(target(dx, dg))
-        def _(position=position):
+        def _(dx=dx, dg=dg):
             for group in groups:
-                for copy in group[position][2]:
+                for copy in group[dx, dg]:
                     copy.wait_send()
 
 
@@ -403,14 +419,10 @@
                 pltpu.SemaphoreType.DMA((copies,))]
     vmem = pl.BlockSpec(memory_space=pltpu.VMEM)
     anywhere = pl.BlockSpec(memory_space=pl.ANY)
-    return pl.pallas_call(
+    shapes = ((n, n, LANES), (n, n, LANES), (mid.n, mid.n, LANES // 2), (coarse.n, coarse.n, LANES // 4))
+    results = pl.pallas_call(
         kernel,
-        out_shape=(
-            jax.ShapeDtypeStruct((n, n, LANES), F32),
-            jax.ShapeDtypeStruct((n, n, LANES), F32),
-            jax.ShapeDtypeStruct((mid.n, mid.n, LANES // 2), F32),
-            jax.ShapeDtypeStruct((coarse.n, coarse.n, LANES // 4), F32),
-        ),
+        out_shape=tuple(pltpu.VMEM(shape, F32) for shape in shapes),
         in_specs=[anywhere, anywhere, anywhere, vmem],
         out_specs=(vmem, vmem, vmem, vmem),
         scratch_shapes=scratch,
@@ -418,6 +430,21 @@
                                              vmem_limit_bytes=56 * 1024 * 1024),
     )(source, conductivity, absorption, brick_mask)
 
+    def deliver(*refs):
+        copies = [pltpu.make_async_copy(refs[i], refs[4 + i], refs[8].at[i]) for i in range(4)]
+        for copy in copies:
+            copy.start()
+        for copy in copies:
+            copy.wait()
+
+    return pl.pallas_call(
+        deliver,
+        out_shape=tuple(jax.ShapeDtypeStruct(shape, F32) for shape in shapes),
+        in_specs=[vmem] * 4,
+        out_specs=(anywhere,) * 4,
+        scratch_shapes=[pltpu.SemaphoreType.DMA((4,))],
+    )(*(pltpu.with_memory_space_constraint(r, pltpu.VMEM) for r in results))
+
 
 def solution(mesh):
     spec = P("dom", "grp", None)

time: 47.2 us -> 36.7 us (0.78)
  Pallas kernels: 42 us -> 35.9 us
  local copies, waits for them, and re-layouts: 4.32 us -> 0 us
    pallas_call x1 -> x2, Pallas kernels: 42 us -> 35.9 us  [the longest x1 34.9 us: step(): pl.pallas_call(kernel, out_shape=tuple((pltpu.VMEM(shape, F32) for shape...]
    unnamed x10 -> x0, local copies, waits for them, and re-layouts: 4.32 us -> none
where the time goes in v3:
time: 36.7 us; the launch traced here: 36.5 us
  Pallas kernels  35.9 us (98%)
  between operations  0.64 us (2%)
    pallas_call x1, Pallas kernels, step(): pl.pallas_call(kernel, out_shape=tuple((pltpu.VMEM(shape, F32) for shape...  34.9 us
    pallas_call x1, Pallas kernels, step(): pl.pallas_call(deliver, out_shape=tuple((jax.ShapeDtypeStruct(shape, F32)...  1.04 us

profile of v3, /device:TPU:25, one launch (start us, length us, event | category | flops | bytes accessed | tf_op | source)
XLA Modules:
  0.0 36.5 jit_solution(17823720785216798905)
XLA Ops:
  0.6 34.9 %shard_map.75 = (f32[32,32,128]{2,1,0:T(8,128)S(1)}, f32[32,32,128]{2,1,0:T(8,128)S(1)}, f32[16,16,64]{2,1,0:T(8,128)S(1)}, f32[8,8,32]{2,1,0:T(8,128)S(1)}) custom-call(f32[32,32,128]{2,1,0:T(8,128)} %refs_0_.1, f32[32,32,128]{2,1,0:T(8,128)} %refs_1_.1, f32[32,32,128]{2,1,0:T(8,128)} %refs_2_.1, s32[4,4,16]{2,1,0:T(4,128)} %refs_3_.1), custom_call_target="tpu_custom_call" | custom-call | tf_op jit(solution)/shard_map/pallas_call | solution.py:423
  35.5 1.0 %shard_map.76 = (f32[32,32,128]{2,1,0:T(8,128)}, f32[32,32,128]{2,1,0:T(8,128)}, f32[16,16,64]{2,1,0:T(8,128)}, f32[8,8,32]{2,1,0:T(8,128)}) custom-call(f32[32,32,128]{2,1,0:T(8,128)S(1)} %get-tuple-element.8.refs_0_, f32[32,32,128]{2,1,0:T(8,128)S(1)} %get-tuple-element.9.refs_1_, f32[16,16,64]{2,1,0:T(8,128)S(1)} %get-tuple-element.10.refs_2_, ...), custom_call_target="tpu_custom_call" | custom-call | tf_op jit(solution)/shard_map/pallas_call | solution.py:440

commit v4 on v3

--- a/solution.py
+++ b/solution.py
@@ -13,7 +13,7 @@
 COARSE_LOW = 0.05
 LANES = 128
 MESH = pl.DeviceIdType.MESH
-DIRS = ((0, 1), (0, -1), (1, 0), (1, 1), (1, -1), (-1, 0), (-1, 1), (-1, -1))
+DIRS = ((-1, 0), (1, 0), (0, 1), (0, -1), (-1, 1), (-1, -1), (1, 1), (1, -1))
 BLOCK = 14
 FAR_FIRST = ((1, 1), (1, -1), (-1, 1), (-1, -1), (1, 0), (-1, 0), (0, 1), (0, -1))
 F32 = jnp.float32
@@ -191,8 +191,8 @@
 
 
 def body_kernel(levels, s_in, k_in, a_in, b_in, it_out, res_out, mid_out, coarse_out,
-                kf, sf, af, km, am, sm, kc, ac, sc, fm, midr, midi, coai,
-                wf, wm, wc, rf, rm, rc, uf, um, uc, local, send, recv):
+                kf, sf, af, pm, sm, pc, sc, bm, fm, midr, midi, coai,
+                wf, wm, wc, rf, rm, rc, uf, um, uc, local, send, recv, beyond):
     fine, mid, coarse = levels
     d, g = lax.axis_index("dom"), lax.axis_index("grp")
     nd, ng = lax.axis_size("dom"), lax.axis_size("grp")
@@ -209,7 +209,7 @@
         return (lax.rem(d + (nd + dx), nd), lax.rem(g + (ng + dg), ng))
 
     barrier = pltpu.get_barrier_semaphore()
-    for dx, dg in DIRS:
+    for dx, dg in DIRS[:4]:
         @pl.when(target(dx, dg))
         def _(dx=dx, dg=dg):
             pl.semaphore_signal(barrier, inc=1, device_id=neighbour(dx, dg), device_id_type=MESH)
@@ -221,9 +221,11 @@
                                      local.at[slot])
         copy.start()
         loads.append(copy)
-
-    fields = ((kf, fine, 1), (af, fine, 0), (sf, fine, 0), (km, mid, 1), (am, mid, 0), (sm, mid, 0),
-              (kc, coarse, 1), (ac, coarse, 0), (sc, coarse, 0))
+    bricks = pltpu.make_async_copy(b_in, bm, local.at[3])
+    bricks.start()
+
+    fields = ((kf, fine, 1), (af, fine, 0), (sf, fine, 0), (pm, mid, 1), (sm, mid, 0),
+              (pc, coarse, 1), (sc, coarse, 0))
     for ref, level, extra in fields:
         w = level.margin + extra
         rows, cells = level.n + 2 * w, level.n
@@ -240,13 +242,69 @@
                     return carry
                 lax.fori_loop(0, rows, clear, 0)
 
+    count_x = low_x.astype(jnp.int32) + high_x.astype(jnp.int32) + 1
+    count_y = low_y.astype(jnp.int32) + high_y.astype(jnp.int32) + 1
+
+    pl.semaphore_wait(barrier, count_x + count_y - 2)
+    for dg in (1, -1):
+        @pl.when(target(0, dg))
+        def _(dg=dg):
+            pl.semaphore_signal(beyond, inc=1, device_id=neighbour(0, dg), device_id_type=MESH)
+
+    used = [0]
+    groups = []
+
+    def halo(parts, order, before_corners=None):
+        group = {}
+        for dx, dg in order:
+            if before_corners is not None and (dx, dg) == DIRS[4]:
+                before_corners()
+            copies = []
+            for ref, level, width, operand in parts:
+                n = level.n
+                deep = width - 1 if dx and dg else width
+                sx, cx = span(dx, n, deep)
+                sy, cy = span(dg, n, deep)
+                if operand is None:
+                    src = ref.at[pl.ds(width + sx, cx), pl.ds(8 + sy, cy), :]
+                else:
+                    src = operand.at[pl.ds(sx, cx), pl.ds(sy, cy), :]
+                slot = used[0]
+                used[0] += 1
+                copies.append(pltpu.make_async_remote_copy(
+                    src_ref=src,
+                    dst_ref=ref.at[pl.ds(landing(dx, n, deep, width), cx),
+                                   pl.ds(landing(dg, n, deep, 8), cy), :],
+                    send_sem=send.at[slot], recv_sem=recv.at[slot],
+                    device_id=neighbour(dx, dg), device_id_type=MESH))
+
+            @pl.when(target(dx, dg))
+            def _(copies=copies):
+                for copy in copies:
+                    copy.start()
+
+            group[dx, dg] = copies
+        groups.append(group)
+        return group
+
+    def arrive(some, signs=(-1, 0, 1)):
+        for dx, dg in DIRS:
+            if dx not in signs:
+                continue
+
+            @pl.when(target(-dx, -dg))
+            def _(dx=dx, dg=dg):
+                for group in some:
+                    for copy in group[dx, dg]:
+                        copy.wait_recv()
+
+    plain_halo = halo(((sf, fine, fine.margin, s_in), (af, fine, fine.margin, a_in)), DIRS,
+                      lambda: pl.semaphore_wait(beyond, count_y - 1))
     lanes_of = (lax.broadcasted_iota(jnp.int32, (16, LANES), 1) // 8
                 == lax.broadcasted_iota(jnp.int32, (16, LANES), 0)).astype(F32)
+    bricks.wait()
     for bx in range(4):
-        fm[pl.ds(8 * bx, 4), :] = jnp.dot(b_in[bx].astype(F32), lanes_of, preferred_element_type=F32)
-
-    count_x = low_x.astype(jnp.int32) + high_x.astype(jnp.int32) + 1
-    count_y = low_y.astype(jnp.int32) + high_y.astype(jnp.int32) + 1
+        fm[pl.ds(8 * bx, 4), :] = jnp.dot(bm[bx].astype(F32), lanes_of, preferred_element_type=F32)
 
     loads[0].wait()
     kx = fine.margin + 1
@@ -260,68 +318,58 @@
         return carry
 
     lax.fori_loop(0, fine.n // 4, mask_own, 0)
+    fine_halo = halo(((kf, fine, kx, None),), DIRS)
     loads[1].wait()
     loads[2].wait()
 
-    pl.semaphore_wait(barrier, count_x * count_y - 1)
-
-    used = [0]
-    groups = []
-
-    def halo(parts, order):
-        group = {}
-        for dx, dg in order:
-            copies = []
-            for ref, level, width in parts:
-                n = level.n
-                sx, cx = span(dx, n, width)
-                sy, cy = span(dg, n, width)
-                slot = used[0]
-                used[0] += 1
-                copies.append(pltpu.make_async_remote_copy(
-                    src_ref=ref.at[pl.ds(width + sx, cx), pl.ds(8 + sy, cy), :],
-                    dst_ref=ref.at[pl.ds(landing(dx, n, width, width), cx),
-                                   pl.ds(landing(dg, n, width, 8), cy), :],
-                    send_sem=send.at[slot], recv_sem=recv.at[slot],
-                    device_id=neighbour(dx, dg), device_id_type=MESH))
-
-            @pl.when(target(dx, dg))
-            def _(copies=copies):
-                for copy in copies:
-                    copy.start()
-
-            group[dx, dg] = copies
-        groups.append(group)
-        return group
-
-    def arrive(group, signs=(-1, 0, 1)):
-        for (dx, dg), copies in group.items():
-            if dx not in signs:
-                continue
-
-            @pl.when(target(-dx, -dg))
-            def _(copies=copies):
-                for copy in copies:
-                    copy.wait_recv()
-
     mx, cx = mid.margin + 1, coarse.margin + 1
-    fine_halo = halo(((kf, fine, kx), (af, fine, fine.margin), (sf, fine, fine.margin)), DIRS)
-
-    def reader(ref, x0, count):
-        return lambda x, y: ref[x + x0, pl.ds(8 + y, count, stride=2), :]
+    lane = lane_index()
+
+    def quad(ref, x, y0, count):
+        lower, upper = pl.ds(y0, count, stride=2), pl.ds(y0 + 1, count, stride=2)
+        return (ref[x, lower, :] + ref[x, upper, :]) + (ref[x + 1, lower, :] + ref[x + 1, upper, :])
+
+    def pack_mid(first, rows):
+        for r in range(rows):
+            x = first + r
+            k = quad(kf, kx + 2 * x, 8, mid.n)
+            a = quad(af, fine.margin + 2 * x, 8, mid.n)
+            pm[mx + x, pl.ds(8, mid.n), :] = 0.125 * jnp.where(
+                lane % 2 == 0, k + pltpu.roll(k, LANES - 1, 1), a + pltpu.roll(a, 1, 1))
+
+    blocks(0, mid.n, pack_mid, 8)
+
+    def pack_coarse(first, rows):
+        for r in range(rows):
+            x = first + r
+            p = quad(pm, mx + 2 * x, 8, coarse.n)
+            q = p + jnp.where(lane % 4 < 2, pltpu.roll(p, LANES - 2, 1), pltpu.roll(p, 2, 1))
+            inner = jnp.where(lane % 4 == 1, pltpu.roll(q, 1, 1), pltpu.roll(q, LANES - 1, 1))
+            outer = jnp.logical_or(lane % 4 == 0, lane % 4 == 3)
+            pc[cx + x, pl.ds(8, coarse.n), :] = 0.125 * jnp.where(outer, q, inner)
+
+    blocks(0, coarse.n, pack_coarse, 8)
+    side_halo = halo(((pm, mid, mx, None), (pc, coarse, cx, None)), DIRS)
+
+    def unpack(ref, level):
+        half = level.stride // 2
+        first = (lane // half) % 2 == 0
+
+        def kappa(x, y):
+            p = ref[x, pl.ds(y, level.ny), :]
+            return jnp.where(first, p, pltpu.roll(p, half, 1))
+
+        def absorb(x, y):
+            p = ref[x + 1, pl.ds(y, level.ny), :]
+            return jnp.where(first, pltpu.roll(p, LANES - half, 1), p)
+
+        return kappa, absorb
 
     def writer(ref, x0, count):
         def write(x, value):
             ref[x + x0, pl.ds(8, count), :] = value
         return write
 
-    pool(reader(kf, kx, mid.n), writer(km, mx, mid.n), mid.n, fine.stride)
-    pool(reader(af, fine.margin, mid.n), writer(am, mid.margin, mid.n), mid.n, fine.stride)
-    pool(reader(km, mx, coarse.n), writer(kc, cx, coarse.n), coarse.n, mid.stride)
-    pool(reader(am, mid.margin, coarse.n), writer(ac, coarse.margin, coarse.n), coarse.n, mid.stride)
-    side_halo = halo(((km, mid, mx), (am, mid, mid.margin), (kc, coarse, cx), (ac, coarse, coarse.margin)),
-                     DIRS)
-
     def at(ref, size):
         return lambda x, y: ref[x, pl.ds(y, size), :]
 
@@ -337,21 +385,22 @@
         sweeps(fine, of(sf), wf, rf, uf, fine_finish, span_of)
 
     edge, end = fine.margin + 1, fine.nx - fine.margin - 1
-    arrive(fine_halo, (0,))
+    fine_groups = (plain_halo, fine_halo)
+    arrive(fine_groups, (0,))
     fine_part(edge, end, lambda k: (edge + 1 + k, end - 1 - k))
-    arrive(fine_halo, (-1,))
+    arrive(fine_groups, (-1,))
     fine_part(end, fine.nx, lambda k: (end - 1 - k, fine.nx - 1 - k))
 
-    arrive(fine_halo, (1,))
+    arrive(fine_groups, (1,))
     fine_part(0, edge, lambda k: (k + 1, edge + 1 + k))
 
     pool(lambda x, y: res_out[x, pl.ds(y, mid.n, stride=2), :], writer(sm, mid.margin, mid.n),
          mid.n, fine.stride)
-    mid_halo = halo(((sm, mid, mid.margin),), FAR_FIRST)
-    arrive(side_halo)
-    setup(mid, at(km, mid.ny), at(am, mid.ny), wm)
-    setup(coarse, at(kc, coarse.ny), at(ac, coarse.ny), wc)
-    arrive(mid_halo)
+    mid_halo = halo(((sm, mid, mid.margin, None),), FAR_FIRST)
+    arrive((side_halo,))
+    setup(mid, *unpack(pm, mid), wm)
+    setup(coarse, *unpack(pc, coarse), wc)
+    arrive((mid_halo,))
     start_iterate(mid, of(sm), wm[4], um[0])
 
     def mid_finish(x, new, total, c, inv):
@@ -362,7 +411,7 @@
 
     pool(lambda x, y: midr[x, pl.ds(y, coarse.n, stride=2), :],
          writer(sc, coarse.margin, coarse.n), coarse.n, mid.stride)
-    coarse_halo = halo(((sc, coarse, coarse.margin),), FAR_FIRST)
+    coarse_halo = halo(((sc, coarse, coarse.margin, None),), FAR_FIRST)
 
     def pick(value, stride):
         cells = LANES // stride
@@ -371,7 +420,7 @@
         return jnp.dot(value, chosen, preferred_element_type=F32, precision=lax.Precision.HIGHEST)
 
     mid_out[...] = pick(midi[...].reshape(mid.n * mid.n, LANES), mid.stride).reshape(mid_out.shape)
-    arrive(coarse_halo)
+    arrive((coarse_halo,))
     start_iterate(coarse, of(sc), wc[4], uc[0])
     a, b = coarse.steps[-1]
 
@@ -400,12 +449,12 @@
     def kernel(*refs):
         body_kernel(levels, *refs)
 
-    fields = []
-    for level in levels:
-        fields += [pltpu.VMEM(level.coefficient_shape(), F32), pltpu.VMEM(level.source_shape(), F32),
-                   pltpu.VMEM(level.source_shape(), F32)]
-    copies = 9 * len(DIRS)
+    fields = [pltpu.VMEM(fine.coefficient_shape(), F32)] + [pltpu.VMEM(fine.source_shape(), F32)] * 2
+    for level in (mid, coarse):
+        fields += [pltpu.VMEM(level.coefficient_shape(), F32), pltpu.VMEM(level.source_shape(), F32)]
+    copies = 7 * len(DIRS)
     scratch = fields + [
+        pltpu.VMEM(brick_mask.shape, jnp.int32),
         pltpu.VMEM((32, LANES), F32),
         pltpu.VMEM((mid.n, mid.n, LANES), F32),
         pltpu.VMEM((mid.n, mid.n, LANES), F32),
@@ -415,15 +464,15 @@
     scratch += [pltpu.VMEM(level.work_shape(), F32) for level in levels]
     scratch += [[pltpu.VMEM(level.work_shape(), F32)] * count
                 for level, count in zip(levels, (DEGREE, DEGREE, COARSE_DEGREE - 1))]
-    scratch += [pltpu.SemaphoreType.DMA((3,)), pltpu.SemaphoreType.DMA((copies,)),
-                pltpu.SemaphoreType.DMA((copies,))]
+    scratch += [pltpu.SemaphoreType.DMA((4,)), pltpu.SemaphoreType.DMA((copies,)),
+                pltpu.SemaphoreType.DMA((copies,)), pltpu.SemaphoreType.REGULAR]
     vmem = pl.BlockSpec(memory_space=pltpu.VMEM)
     anywhere = pl.BlockSpec(memory_space=pl.ANY)
     shapes = ((n, n, LANES), (n, n, LANES), (mid.n, mid.n, LANES // 2), (coarse.n, coarse.n, LANES // 4))
     results = pl.pallas_call(
         kernel,
         out_shape=tuple(pltpu.VMEM(shape, F32) for shape in shapes),
-        in_specs=[anywhere, anywhere, anywhere, vmem],
+        in_specs=[anywhere] * 4,
         out_specs=(vmem, vmem, vmem, vmem),
         scratch_shapes=scratch,
         compiler_params=pltpu.CompilerParams(collective_id=0, has_side_effects=True,

time: 36.7 us -> 32.9 us (0.90)
  Pallas kernels: 35.9 us -> 32 us
    pallas_call x1, Pallas kernels: 34.9 us -> 31 us  [step(): pl.pallas_call(kernel, out_shape=tuple((pltpu.VMEM(shape, F32) for shape...]
where the time goes in v4:
time: 32.9 us; the launch traced here: 32.7 us
  Pallas kernels  32 us (97%)
  between operations  0.64 us (2%)
    pallas_call x1, Pallas kernels, step(): pl.pallas_call(kernel, out_shape=tuple((pltpu.VMEM(shape, F32) for shape...  31 us
    pallas_call x1, Pallas kernels, step(): pl.pallas_call(deliver, out_shape=tuple((jax.ShapeDtypeStruct(shape, F32)...  1.04 us

profile of v4, /device:TPU:25, one launch (start us, length us, event | category | flops | bytes accessed | tf_op | source)
XLA Modules:
  0.0 32.7 jit_solution(12193893354773074081)
XLA Ops:
  0.6 31.0 %shard_map.75 = (f32[32,32,128]{2,1,0:T(8,128)S(1)}, f32[32,32,128]{2,1,0:T(8,128)S(1)}, f32[16,16,64]{2,1,0:T(8,128)S(1)}, f32[8,8,32]{2,1,0:T(8,128)S(1)}) custom-call(f32[32,32,128]{2,1,0:T(8,128)} %refs_0_.1, f32[32,32,128]{2,1,0:T(8,128)} %refs_1_.1, f32[32,32,128]{2,1,0:T(8,128)} %refs_2_.1, s32[4,4,16]{2,1,0:T(4,128)} %refs_3_.1), custom_call_target="tpu_custom_call" | custom-call | tf_op jit(solution)/shard_map/pallas_call | solution.py:472
  31.6 1.0 %shard_map.76 = (f32[32,32,128]{2,1,0:T(8,128)}, f32[32,32,128]{2,1,0:T(8,128)}, f32[16,16,64]{2,1,0:T(8,128)}, f32[8,8,32]{2,1,0:T(8,128)}) custom-call(f32[32,32,128]{2,1,0:T(8,128)S(1)} %get-tuple-element.8.refs_0_, f32[32,32,128]{2,1,0:T(8,128)S(1)} %get-tuple-element.9.refs_1_, f32[16,16,64]{2,1,0:T(8,128)S(1)} %get-tuple-element.10.refs_2_, ...), custom_call_target="tpu_custom_call" | custom-call | tf_op jit(solution)/shard_map/pallas_call | solution.py:489

commit v5 on v4

--- a/solution.py
+++ b/solution.py
@@ -93,15 +93,16 @@
             other = jnp.where(even, pltpu.roll(p, LANES - stride, 1), pltpu.roll(p, stride, 1))
             write(first + i, (p + other) * 0.125)
 
-    blocks(0, count, body)
-
-
-def setup(level, kappa, absorb, work, source=None, u0=None, span_x=None):
+    blocks(0, count, body, count)
+
+
+def setup(level, kappa, absorb, work, source=None, u0=None, span_x=None, span_y=None):
     wx, wy, wz, diag, inv = work
     half = level.scale * 0.5
     up = lane_index() < LANES - level.stride
     down = lane_index() >= level.stride
-    y0, ny = level.y0, level.ny
+    skip, ny = span_y or (0, level.ny)
+    y0 = level.y0 + skip
 
     def flag(k):
         return jnp.where(k > 0.0, 1.0, 0.0)
@@ -118,7 +119,7 @@
             total = (xp + xm) + (yp + ym) + (zp + zm)
             count = (flags[r + 2] + flags[r]) + (flag(yp) + flag(ym)) + (flag(zp) + flag(zm))
             d = (1.0 + half * (k * count + total)) + level.scale * absorb(i, y0) * (6.0 - count)
-            at = pl.ds(8, ny)
+            at = pl.ds(8 + skip, ny)
             wx[i, at, :] = half * (k + xp)
             wy[i, at, :] = half * (k + yp)
             wz[i, at, :] = jnp.where(up, half * (k + zp), 0.0)
@@ -224,12 +225,14 @@
     bricks = pltpu.make_async_copy(b_in, bm, local.at[3])
     bricks.start()
 
-    fields = ((kf, fine, 1), (af, fine, 0), (sf, fine, 0), (pm, mid, 1), (sm, mid, 0),
-              (pc, coarse, 1), (sc, coarse, 0))
-    for ref, level, extra in fields:
-        w = level.margin + extra
-        rows, cells = level.n + 2 * w, level.n
-        for missing, x0 in ((d == 0, 0), (d == nd - 1, w + cells)):
+    fields = ((kf, fine, 1, False), (af, fine, 0, False), (sf, fine, 0, False), (pm, mid, 1, False),
+              (sm, mid, 0, True), (pc, coarse, 1, False), (sc, coarse, 0, True))
+    for ref, level, extra, paired in fields:
+        w, deep, cells = level.margin + extra, level.n, level.n
+        if paired:
+            w, deep = (w + 1) // 2, cells // 2
+        rows = deep + 2 * w
+        for missing, x0 in ((d == 0, 0), (d == nd - 1, w + deep)):
             @pl.when(missing)
             def _(ref=ref, level=level, w=w, x0=x0):
                 for x in range(w):
@@ -260,20 +263,23 @@
             if before_corners is not None and (dx, dg) == DIRS[4]:
                 before_corners()
             copies = []
-            for ref, level, width, operand in parts:
+            for ref, level, width, operand, paired in parts:
                 n = level.n
                 deep = width - 1 if dx and dg else width
-                sx, cx = span(dx, n, deep)
+                rows, border, deep_x = n, width, deep
+                if paired:
+                    rows, border, deep_x = n // 2, (width + 1) // 2, (deep + 1) // 2
+                sx, cx = span(dx, rows, deep_x)
                 sy, cy = span(dg, n, deep)
                 if operand is None:
-                    src = ref.at[pl.ds(width + sx, cx), pl.ds(8 + sy, cy), :]
+                    src = ref.at[pl.ds(border + sx, cx), pl.ds(8 + sy, cy), :]
                 else:
                     src = operand.at[pl.ds(sx, cx), pl.ds(sy, cy), :]
                 slot = used[0]
                 used[0] += 1
                 copies.append(pltpu.make_async_remote_copy(
                     src_ref=src,
-                    dst_ref=ref.at[pl.ds(landing(dx, n, deep, width), cx),
+                    dst_ref=ref.at[pl.ds(landing(dx, rows, deep_x, border), cx),
                                    pl.ds(landing(dg, n, deep, 8), cy), :],
                     send_sem=send.at[slot], recv_sem=recv.at[slot],
                     device_id=neighbour(dx, dg), device_id_type=MESH))
@@ -298,7 +304,7 @@
                     for copy in group[dx, dg]:
                         copy.wait_recv()
 
-    plain_halo = halo(((sf, fine, fine.margin, s_in), (af, fine, fine.margin, a_in)), DIRS,
+    plain_halo = halo(((sf, fine, fine.margin, s_in, False), (af, fine, fine.margin, a_in, False)), DIRS,
                       lambda: pl.semaphore_wait(beyond, count_y - 1))
     lanes_of = (lax.broadcasted_iota(jnp.int32, (16, LANES), 1) // 8
                 == lax.broadcasted_iota(jnp.int32, (16, LANES), 0)).astype(F32)
@@ -318,7 +324,7 @@
         return carry
 
     lax.fori_loop(0, fine.n // 4, mask_own, 0)
-    fine_halo = halo(((kf, fine, kx, None),), DIRS)
+    fine_halo = halo(((kf, fine, kx, None, False),), DIRS)
     loads[1].wait()
     loads[2].wait()
 
@@ -349,7 +355,7 @@
             pc[cx + x, pl.ds(8, coarse.n), :] = 0.125 * jnp.where(outer, q, inner)
 
     blocks(0, coarse.n, pack_coarse, 8)
-    side_halo = halo(((pm, mid, mx, None), (pc, coarse, cx, None)), DIRS)
+    side_halo = halo(((pm, mid, mx, None, False), (pc, coarse, cx, None, False)), DIRS)
 
     def unpack(ref, level):
         half = level.stride // 2
@@ -365,10 +371,26 @@
 
         return kappa, absorb
 
-    def writer(ref, x0, count):
+    def paired_rows(ref, level):
+        half = level.stride // 2
+        first = (lane // half) % 2 == 0
+        border = (level.margin + 1) // 2
+        held = []
+
         def write(x, value):
-            ref[x + x0, pl.ds(8, count), :] = value
-        return write
+            held.append(value)
+            if x % 2 == 1:
+                odd, even = held.pop(), held.pop()
+                ref[border + x // 2, pl.ds(8, level.n), :] = jnp.where(first, even, odd)
+
+        def read(i, y, size):
+            q = i + 2 * border - level.margin
+            p = ref[q // 2, pl.ds(y, size), :]
+            if q % 2 == 0:
+                return jnp.where(first, p, pltpu.roll(p, half, 1))
+            return jnp.where(first, pltpu.roll(p, LANES - half, 1), p)
+
+        return write, read
 
     def at(ref, size):
         return lambda x, y: ref[x, pl.ds(y, size), :]
@@ -380,38 +402,45 @@
         it_out[x] = total
         res_out[x] = jnp.where(inv > 0.0, new, 0.0)
 
-    def fine_part(low, high, span_of):
-        setup(fine, at(kf, fine.ny), at(af, fine.ny), wf, of(sf), uf[0], (low, high))
+    def fine_setup(low, high, skip, size):
+        setup(fine, at(kf, size), at(af, size), wf, of(sf), uf[0], (low, high), (skip, size))
+
+    def fine_part(low, high, span_of, ready=False):
+        if not ready:
+            fine_setup(low, high, 0, fine.ny)
         sweeps(fine, of(sf), wf, rf, uf, fine_finish, span_of)
 
     edge, end = fine.margin + 1, fine.nx - fine.margin - 1
     fine_groups = (plain_halo, fine_halo)
+    fine_setup(edge, end, 8, fine.ny - 16)
     arrive(fine_groups, (0,))
-    fine_part(edge, end, lambda k: (edge + 1 + k, end - 1 - k))
+    fine_setup(edge, end, 0, 8)
+    fine_setup(edge, end, fine.ny - 8, 8)
+    fine_part(edge, end, lambda k: (edge + 1 + k, end - 1 - k), ready=True)
+
     arrive(fine_groups, (-1,))
     fine_part(end, fine.nx, lambda k: (end - 1 - k, fine.nx - 1 - k))
-
     arrive(fine_groups, (1,))
     fine_part(0, edge, lambda k: (k + 1, edge + 1 + k))
 
-    pool(lambda x, y: res_out[x, pl.ds(y, mid.n, stride=2), :], writer(sm, mid.margin, mid.n),
-         mid.n, fine.stride)
-    mid_halo = halo(((sm, mid, mid.margin, None),), FAR_FIRST)
+    put, mid_source = paired_rows(sm, mid)
+    pool(lambda x, y: res_out[x, pl.ds(y, mid.n, stride=2), :], put, mid.n, fine.stride)
+    mid_halo = halo(((sm, mid, mid.margin, None, True),), FAR_FIRST)
     arrive((side_halo,))
     setup(mid, *unpack(pm, mid), wm)
     setup(coarse, *unpack(pc, coarse), wc)
     arrive((mid_halo,))
-    start_iterate(mid, of(sm), wm[4], um[0])
+    start_iterate(mid, mid_source, wm[4], um[0])
 
     def mid_finish(x, new, total, c, inv):
         midi[x] = total
         midr[x] = jnp.where(inv > 0.0, new, 0.0)
 
-    sweeps(mid, of(sm), wm, rm, um, mid_finish)
-
-    pool(lambda x, y: midr[x, pl.ds(y, coarse.n, stride=2), :],
-         writer(sc, coarse.margin, coarse.n), coarse.n, mid.stride)
-    coarse_halo = halo(((sc, coarse, coarse.margin, None),), FAR_FIRST)
+    sweeps(mid, mid_source, wm, rm, um, mid_finish)
+
+    put, coarse_source = paired_rows(sc, coarse)
+    pool(lambda x, y: midr[x, pl.ds(y, coarse.n, stride=2), :], put, coarse.n, mid.stride)
+    coarse_halo = halo(((sc, coarse, coarse.margin, None, True),), FAR_FIRST)
 
     def pick(value, stride):
         cells = LANES // stride
@@ -421,13 +450,13 @@
 
     mid_out[...] = pick(midi[...].reshape(mid.n * mid.n, LANES), mid.stride).reshape(mid_out.shape)
     arrive((coarse_halo,))
-    start_iterate(coarse, of(sc), wc[4], uc[0])
+    start_iterate(coarse, coarse_source, wc[4], uc[0])
     a, b = coarse.steps[-1]
 
     def coarse_finish(x, new, total, c, inv):
         coai[x] = total + (a * c + b * (inv * new))
 
-    sweeps(coarse, of(sc), wc, rc, uc, coarse_finish)
+    sweeps(coarse, coarse_source, wc, rc, uc, coarse_finish)
     coarse_out[...] = pick(coai[...].reshape(coarse.n * coarse.n, LANES),
                            coarse.stride).reshape(coarse_out.shape)
 
@@ -451,7 +480,8 @@
 
     fields = [pltpu.VMEM(fine.coefficient_shape(), F32)] + [pltpu.VMEM(fine.source_shape(), F32)] * 2
     for level in (mid, coarse):
-        fields += [pltpu.VMEM(level.coefficient_shape(), F32), pltpu.VMEM(level.source_shape(), F32)]
+        pairs = level.n // 2 + 2 * ((level.margin + 1) // 2)
+        fields += [pltpu.VMEM(level.coefficient_shape(), F32), pltpu.VMEM((pairs, level.yb, LANES), F32)]
     copies = 7 * len(DIRS)
     scratch = fields + [
         pltpu.VMEM(brick_mask.shape, jnp.int32),

time: 32.9 us -> 32.7 us (level)
  no operation moved by 1% of the time
where the time goes in v5:
time: 32.7 us; the launch traced here: 32.5 us
  Pallas kernels  31.9 us (98%)
  between operations  0.64 us (2%)
    pallas_call x1, Pallas kernels, step(): pl.pallas_call(kernel, out_shape=tuple((pltpu.VMEM(shape, F32) for shape...  30.8 us
    pallas_call x1, Pallas kernels, step(): pl.pallas_call(deliver, out_shape=tuple((jax.ShapeDtypeStruct(shape, F32)...  1.04 us

profile of v5, /device:TPU:25, one launch (start us, length us, event | category | flops | bytes accessed | tf_op | source)
XLA Modules:
  0.0 32.5 jit_solution(3764807220361604024)
XLA Ops:
  0.6 30.8 %shard_map.75 = (f32[32,32,128]{2,1,0:T(8,128)S(1)}, f32[32,32,128]{2,1,0:T(8,128)S(1)}, f32[16,16,64]{2,1,0:T(8,128)S(1)}, f32[8,8,32]{2,1,0:T(8,128)S(1)}) custom-call(f32[32,32,128]{2,1,0:T(8,128)} %refs_0_.1, f32[32,32,128]{2,1,0:T(8,128)} %refs_1_.1, f32[32,32,128]{2,1,0:T(8,128)} %refs_2_.1, s32[4,4,16]{2,1,0:T(4,128)} %refs_3_.1), custom_call_target="tpu_custom_call" | custom-call | tf_op jit(solution)/shard_map/pallas_call | solution.py:502
  31.5 1.0 %shard_map.76 = (f32[32,32,128]{2,1,0:T(8,128)}, f32[32,32,128]{2,1,0:T(8,128)}, f32[16,16,64]{2,1,0:T(8,128)}, f32[8,8,32]{2,1,0:T(8,128)}) custom-call(f32[32,32,128]{2,1,0:T(8,128)S(1)} %get-tuple-element.8.refs_0_, f32[32,32,128]{2,1,0:T(8,128)S(1)} %get-tuple-element.9.refs_1_, f32[16,16,64]{2,1,0:T(8,128)S(1)} %get-tuple-element.10.refs_2_, ...), custom_call_target="tpu_custom_call" | custom-call | tf_op jit(solution)/shard_map/pallas_call | solution.py:519
